TPU v7x, 128 devices: a whole 4x4x4 slice. The times are simulated.
128 devices in a mesh: dp: 4 (over z_lo, core), seq: 32 (over z_hi, y, x).
Axes of the slice: x: 4, y: 4, z: 4 (z_hi: 2, z_lo: 2; z = z_hi * 2 + z_lo), core: 2. Of those that a mesh axis runs over, the one named last changes fastest.
Arguments:
- tokens: bfloat16 [4, 4096, 2048], P('dp', 'seq'), may hold values from -40 to 40
- cotangent: bfloat16 [4, 4096, 2048], P('dp', 'seq'), may hold values from -6 to 6
- w_qkv: bfloat16 [2048, 3072], replicated
- w_out: bfloat16 [2048, 1024], replicated, may hold values from -0.1875 to 0.1875
- key_blocks: int32 [32, 3], replicated, may hold values from 0 to 31, as said below
- key_count: int32 [32], replicated, may hold values from 1 to 3, as said below
Outputs:
- layer_out: bfloat16 [4, 4096, 2048], P('dp', 'seq')
- grad_tokens: bfloat16 [4, 4096, 2048], P('dp', 'seq')
- grad_w_qkv: float32 [2048, 3072], P('seq')
- grad_w_out: float32 [2048, 1024], P('seq')
Inputs may be any that keep to these rules, and one draw needn't show every extreme that they name: Query block b uses the first key_count[b] entries of row b of key_blocks; 3 is reached in every draw. `key_blocks`: the first key_count[b] entries of row b are distinct; every entry e of row b satisfies |e - b| <= 1; among its used entries, the last block of every run of 1 block lists the block after it and the first block of every run lists the block before it, where those exist.
All inputs are finite; a program needn't handle non-finite values.
Results may differ from a plain program's by a relative error of at most 0.034.
Values may be sent and summed in bfloat16 or wider, within the bound.
A program may use at most 128 MiB of HBM per device.

v0:
```python
import math

import jax
import jax.numpy as jnp
from jax import lax
from jax.sharding import PartitionSpec as P

LOCAL_HEADS = 8
HEAD = 128
MASK_BLOCK_SIZE = 128
TOK_DEV = 128


epsilon = 1e-06


def padded(array, sides, width):
    for axis, dim in sides:
        size, length = (lax.axis_size(axis), array.shape[dim])
        up = [(i, (i + 1) % size) for i in range(size - 1)]
        down = [(j, i) for i, j in up]
        last = lax.slice_in_dim(array, length - width, length, axis=dim)
        leading = lax.slice_in_dim(array, 0, width, axis=dim)
        before = lax.ppermute(last, axis, up)
        after = lax.ppermute(leading, axis, down)
        array = jnp.concatenate([before, array, after], axis=dim)
    return array


def shifted(value, axis, steps):
    count = lax.axis_size(axis)
    leading, last = (max(0, -steps), min(count, count - steps))
    return lax.ppermute(value, axis, [(source, source + steps) for source in range(leading, last)])


def block_view(matrix):
    return matrix.reshape(matrix.shape[0] // MASK_BLOCK_SIZE, MASK_BLOCK_SIZE, LOCAL_HEADS, HEAD)


def visit_plan(counts, step):
    ends = jnp.cumsum(counts)
    slot = jnp.sum((step >= ends).astype(jnp.int32))
    visit = step - (ends[slot] - counts[slot])
    return (slot, visit)


def pair_scores(query_block_rows, key_window, listed, window_start, slot, visit):
    local_id = listed[slot, visit] - window_start
    key_rows = key_window[local_id]
    scores = jnp.einsum(
        "qhe,khe->hqk", query_block_rows[slot], key_rows, preferred_element_type=jnp.float32
    ) * HEAD ** (-0.5)
    return (scores, local_id, key_rows)


def attend_forward(query_slots, window, listed, counts, window_start):
    inner = LOCAL_HEADS * HEAD
    query_block_rows = block_view(query_slots)
    key_window = block_view(window[:, :inner])
    value_window = block_view(window[:, inner:])
    total_pairs = jnp.sum(counts)
    slot_count = query_block_rows.shape[0]

    def first_pass(step, carry):
        running_max, partial_sum_state = carry
        slot, visit = visit_plan(counts, step)
        scores, local_id, key_rows = pair_scores(
            query_block_rows, key_window, listed, window_start, slot, visit
        )
        old_max = running_max[slot]
        new_max = jnp.maximum(old_max, jnp.max(scores, axis=2))
        new_sum = partial_sum_state[slot] * jnp.exp(old_max - new_max) + jnp.sum(
            jnp.exp(scores - new_max[..., None]), axis=2
        )
        return (running_max.at[slot].set(new_max), partial_sum_state.at[slot].set(new_sum))

    start_state = (
        jnp.full((slot_count, LOCAL_HEADS, MASK_BLOCK_SIZE), -jnp.inf, jnp.float32),
        jnp.zeros((slot_count, LOCAL_HEADS, MASK_BLOCK_SIZE), jnp.float32),
    )
    running_max, partial_sum_state = lax.fori_loop(0, total_pairs, first_pass, start_state)
    log_totals = running_max + jnp.log(partial_sum_state)

    def second_pass(step, accumulated):
        slot, visit = visit_plan(counts, step)
        scores, local_id, key_rows = pair_scores(
            query_block_rows, key_window, listed, window_start, slot, visit
        )
        weights = jnp.exp(scores - log_totals[slot][..., None]).astype(jnp.bfloat16)
        contribution = jnp.einsum(
            "hqk,khe->qhe", weights, value_window[local_id], preferred_element_type=jnp.float32
        )
        return accumulated.at[slot].add(contribution)

    accumulated = lax.fori_loop(
        0, total_pairs, second_pass, jnp.zeros(query_block_rows.shape, jnp.float32)
    )
    return (accumulated.reshape(query_slots.shape).astype(jnp.bfloat16), log_totals)


def attend_backward(
    query_slots, window, listed, counts, window_start, log_totals, attended_slots, grad_slots
):
    inner = LOCAL_HEADS * HEAD
    query_block_rows = block_view(query_slots)
    key_window = block_view(window[:, :inner])
    value_window = block_view(window[:, inner:])
    grad_blocks = block_view(grad_slots)
    total_pairs = jnp.sum(counts)
    row_delta = jnp.sum(
        grad_blocks.astype(jnp.float32) * block_view(attended_slots).astype(jnp.float32), axis=3
    )
    row_delta = jnp.transpose(row_delta, (0, 2, 1))

    def back_pass(step, carry):
        grad_query, grad_keys, grad_values = carry
        slot, visit = visit_plan(counts, step)
        scores, local_id, key_rows = pair_scores(
            query_block_rows, key_window, listed, window_start, slot, visit
        )
        probability = jnp.exp(scores - log_totals[slot][..., None])
        weights = probability.astype(jnp.bfloat16)
        grad_rows = grad_blocks[slot]
        grad_values = grad_values.at[local_id].add(
            jnp.einsum("hqk,qhe->khe", weights, grad_rows, preferred_element_type=jnp.float32)
        )
        grad_prob = jnp.einsum(
            "qhe,khe->hqk", grad_rows, value_window[local_id], preferred_element_type=jnp.float32
        )
        score_gradient = (
            probability * (grad_prob - row_delta[slot][..., None]) * HEAD ** (-0.5)
        ).astype(jnp.bfloat16)
        grad_query = grad_query.at[slot].add(
            jnp.einsum("hqk,khe->qhe", score_gradient, key_rows, preferred_element_type=jnp.float32)
        )
        grad_keys = grad_keys.at[local_id].add(
            jnp.einsum(
                "hqk,qhe->khe",
                score_gradient,
                query_block_rows[slot],
                preferred_element_type=jnp.float32,
            )
        )
        return (grad_query, grad_keys, grad_values)

    window_zeros = jnp.zeros(key_window.shape, jnp.float32)
    start_state = (jnp.zeros(query_block_rows.shape, jnp.float32), window_zeros, window_zeros)
    grad_query, grad_keys, grad_values = lax.fori_loop(0, total_pairs, back_pass, start_state)
    window_rows = key_window.shape[0] * MASK_BLOCK_SIZE
    grad_window = jnp.concatenate(
        [grad_keys.reshape(window_rows, inner), grad_values.reshape(window_rows, inner)], axis=1
    )
    return (grad_query.reshape(query_slots.shape).astype(jnp.bfloat16), grad_window)


def body(tokens, cotangent, w_qkv, w_out, key_blocks, key_count):
    inner = LOCAL_HEADS * HEAD
    blocks_dev = TOK_DEV // MASK_BLOCK_SIZE
    seq_devices = lax.axis_size("seq")
    position = lax.axis_index("seq")
    total_tokens = lax.axis_size("dp") * seq_devices * TOK_DEV
    factor = 1.0 / math.sqrt(total_tokens)
    contract_rows = (((0,), (0,)), ((), ()))
    contract_columns = (((1,), (1,)), ((), ()))
    wide_tokens = tokens[0].astype(jnp.float32)
    upstream = cotangent[0]
    inv_rms = lax.rsqrt(jnp.mean(wide_tokens * wide_tokens, axis=1, keepdims=True) + epsilon)
    normed_wide = wide_tokens * inv_rms
    normed = normed_wide.astype(jnp.bfloat16)
    qkv = jnp.dot(normed, w_qkv, preferred_element_type=jnp.float32).astype(jnp.bfloat16)
    query = qkv[:, :inner]
    key_value = qkv[:, inner:]
    own_first = position * blocks_dev
    own_ids = own_first + jnp.arange(blocks_dev, dtype=jnp.int32)
    window = padded(key_value, (("seq", 0),), TOK_DEV)
    window_start = (position - 1) * blocks_dev
    listed = key_blocks[own_ids]
    counts = key_count[own_ids]
    attended_slots, log_totals = attend_forward(query, window, listed, counts, window_start)
    out_proj = lax.dot_general(
        attended_slots, w_out, contract_columns, preferred_element_type=jnp.float32
    )
    layer_out = (wide_tokens + out_proj).astype(jnp.bfloat16)
    grad_att = jnp.dot(upstream, w_out, preferred_element_type=jnp.float32).astype(jnp.bfloat16)
    grad_query, grad_window = attend_backward(
        query, window, listed, counts, window_start, log_totals, attended_slots, grad_att
    )
    grad_kv = grad_window[TOK_DEV : 2 * TOK_DEV]
    for offset in (-1, 1):
        outgoing = grad_window[(offset + 1) * TOK_DEV : (offset + 2) * TOK_DEV]
        grad_kv = grad_kv + shifted(outgoing.astype(jnp.bfloat16), "seq", offset).astype(
            outgoing.dtype
        )
    grad_qkv = jnp.concatenate([grad_query, grad_kv.astype(jnp.bfloat16)], axis=1)
    grad_normed = lax.dot_general(
        grad_qkv, w_qkv, contract_columns, preferred_element_type=jnp.float32
    )
    branch_choice = inv_rms * (
        grad_normed - normed_wide * jnp.mean(grad_normed * normed_wide, axis=1, keepdims=True)
    )
    grad_tokens = (upstream.astype(jnp.float32) + branch_choice).astype(jnp.bfloat16)
    term_qkv = lax.dot_general(normed, grad_qkv, contract_rows, preferred_element_type=jnp.float32)
    term_out = lax.dot_general(
        upstream, attended_slots, contract_rows, preferred_element_type=jnp.float32
    )
    shares = lax.psum_scatter(
        jnp.concatenate([term_qkv, term_out], axis=1).astype(jnp.bfloat16),
        "seq",
        scatter_dimension=0,
        tiled=True,
    )
    summed = lax.psum(shares, "dp").astype(jnp.float32) * factor
    grad_w_qkv = summed[:, : 3 * inner]
    grad_w_out = summed[:, 3 * inner :]
    return (layer_out[None], grad_tokens[None], grad_w_qkv, grad_w_out)


def solution(mesh):
    return jax.shard_map(
        body,
        mesh=mesh,
        in_specs=(P("dp", "seq", None), P("dp", "seq", None), P(), P(), P(), P()),
        out_specs=(P("dp", "seq", None), P("dp", "seq", None), P("seq", None), P("seq", None)),
        check_vma=False,
    )
```

profile of v0, /device:TPU:1, one launch (start us, length us, event | category | flops | bytes accessed | tf_op | source)
XLA Modules:
  0.0 423.7 jit_solution(15402971528699469692)
XLA Ops:
  7.2 1.2 fusion.55
  8.5 6.7 %convolution_convert_fusion.1 = bf16[128,3072]{1,0:T(8,128)(2,1)S(1)} fusion(bf16[2048,3072]{1,0:T(8,128)(2,1)} %param.26, bf16[1,128,2048]{2,1,0:T(8,128)(2,1)} %param.24, f32[128]{0:T(128)S(1)} %add_rsqrt_fusion), kind=kOutput, calls=%fused_computation.78 | convolution fusion | flops 1611792384 | bytes 13894144 | tf_op jit(solution)/shard_map/dot_general | solution.py:170
  15.2 1.3 collective-permute-start.1
  16.5 4.6 %collective-permute-start = (bf16[128,2048]{1,0:T(8,128)(2,1)S(1)}, bf16[128,2048]{1,0:T(8,128)(2,1)S(1)}, u32[]{:S(2)}, u32[]{:S(2)}) collective-permute-start(bf16[128,2048]{1,0:T(8,128)(2,1)S(1)} %slice.186), channel_id=1, source_target_pairs={{0,1},{1,2},{2,3},{3,4},{4,5},{5,6},{6,7},{7,8},{8,9},{9,10},{10,1... | collective-permute-start | bytes 1572872 | tf_op jit(solution)/shard_map/ppermute | solution.py:24
  21.2 2.9 fusion.49
  24.2 0.9 copy.27
  26.0 0.8 copy.55
  26.7 1.0 copy.25
  27.7 2.6 collective-permute-done.1
  30.3 0.9 collective-permute-done
  31.6 0.9 copy-done.7
  32.7 9.2 %while.53 = (s32[]{:T(128)}, f32[1,8,128]{2,1,0:T(8,128)S(1)}, f32[1,8,128]{2,1,0:T(8,128)S(1)}, s32[]{:T(128)}, s32[1,1]{1,0:T(1,128)}, /*index=5*/s32[1,3]{1,0...) while((s32[]{:T(128)}, f32[1,8,128]{2,1,0:T(8,128)S(1)}, ...), condition=%wide.region_5.6_spmd, body=%wide.region_1.5_spmd.sunk | while | flops 34083864 | bytes 1622303 | solution.py:81
  42.1 13.7 %while.54 = (s32[]{:T(128)}, f32[1,128,8,128]{1,3,2,0:T(8,128)S(1)}, s32[]{:T(128)}, s32[1,1]{1,0:T(1,128)}, s32[1,3]{1,0:T(1,128)S(1)}, /*index=5*/s32[]{:T(128...) while((s32[]{:T(128)}, ...), condition=%wide.region_8.9_spmd, body=%wide.region_6.0_spmd.sunk | while | flops 67764264 | bytes 3412267 | solution.py:95
  45.4 1.0 dynamic-slice_bitcast_fusion.2
  46.6 2.0 fusion.101
  51.9 1.0 dynamic-slice_bitcast_fusion.2
  53.2 2.0 fusion.101
  55.9 2.0 multiply_reduce_fusion
  58.0 1.3 broadcast_in_dim.32.clone
  59.2 20.7 %while.55 = (s32[]{:T(128)}, f32[1,128,8,128]{1,3,2,0:T(8,128)S(1)}, f32[3,128,8,128]{3,2,1,0:T(8,128)}, f32[3,128,8,128]{3,2,1,0:T(8,128)S(1)}, s32[]{:T(128)},...) while((s32[]{:T(128)}, ...), condition=%wide.region_13.14_spmd, body=%wide.region_10.13_spmd.sunk | while | flops 169476160 | bytes 24650164 | solution.py:148
  63.2 1.0 constant_dynamic-slice_fusion.19
  64.8 0.9 fusion.113
  65.8 0.8 fusion.115
  66.6 0.8 fusion.114
  68.1 1.1 copy-done.4
  73.2 1.0 constant_dynamic-slice_fusion.19
  74.8 0.9 fusion.113
  75.8 0.8 fusion.115
  76.6 0.8 fusion.114
  78.1 1.1 copy-done.4
  79.9 1.7 bitcast_dynamic-update-slice_fusion.1
  82.3 1.0 fusion.67
  84.0 1.3 collective-permute-start.2
  85.3 25.8 %collective-permute-start.3 = (bf16[128,2048]{1,0:T(8,128)(2,1)}, bf16[128,2048]{1,0:T(8,128)(2,1)S(1)}, u32[]{:S(2)}, u32[]{:S(2)}) collective-permute-start(bf16[128,2048]{1,0:T(8,128)(2,1)} %get-tuple-element.755), channel_id=1, source_target_pairs={{0,1},{1,2},{2,3},{3,4},{4,5},{5,6},{6,7},{7,8},{8,9},{9,10},{10,1... | collective-permute-start | bytes 1572872 | tf_op jit(solution)/shard_map/ppermute | solution.py:33
  111.3 3.2 convert_bitcast_fusion
  114.6 4.8 %collective-permute-done.2 = bf16[128,2048]{1,0:T(8,128)(2,1)S(1)} collective-permute-done((bf16[128,2048]{1,0:T(8,128)(2,1)}, bf16[128,2048]{1,0:T(8,128)(2,1)S(1)}, u32[]{:S(2)}, u32[]{:S(2)}) %collective-permute-start.2) | collective-permute-done | bytes 524320 | tf_op jit(solution)/shard_map/ppermute | solution.py:33
  119.4 1.0 collective-permute-done.3
  120.4 1.4 fusion.57
  121.8 3.9 convolution_convert_fusion
  125.7 9.2 %pad_maximum_fusion = bf16[2048,4096]{1,0:T(8,128)(2,1)} fusion(bf16[2048,1024]{1,0:T(8,128)(2,1)} %convert_bitcast_fusion, bf16[2048,3072]{1,0:T(8,128)(2,1)S(1)} %convolution_convert_fusion), kind=kLoop, calls=%fused_computation.75 | loop fusion | flops 33554432 | bytes 33554432 | tf_op jit(solution)/shard_map/concatenate | solution.py:207
  135.0 4.5 %fusion.45 = bf16[1,128,2048]{2,1,0:T(8,128)(2,1)} fusion(bf16[128,1024]{0,1:T(8,128)(2,1)S(1)} %bitcast.242, bf16[2048,1024]{1,0:T(8,128)(2,1)} %param.27, bf16[1,128,2048]{2,1,0:T(8,128)(2,1)S(1)} %copy-done.2), kind=kOutput, calls=%fused_computation.81 | convolution fusion | flops 537657344 | bytes 5505024 | tf_op jit(solution)/shard_map/dot_general | solution.py:180
  139.5 8.9 %fusion.50 = (f32[128]{0:T(128)S(1)}, f32[128,2048]{1,0:T(8,128)S(1)}) fusion(bf16[1,128,2048]{2,1,0:T(8,128)(2,1)S(1)} %copy-done.2, f32[128]{0:T(128)S(1)} %add_rsqrt_fusion, bf16[2048,3072]{1,0:T(8,128)(2,1)} %param.26, bf16[128,2048]{1,0:T(8,128)(2,1)S(1)} %fusion.57, bf16[128,1024]{1,0:T(8,128)(2,1)S(1)} %copy.40), kind=kOutput, calls=%fused_computation.92 | convolution fusion | flops 1613234048 | bytes 14943232 | tf_op jit(solution)/shard_map/dot_general | solution.py:195
  148.4 207.9 %reduce-scatter.2.cloned.1.call-done = bf16[64,4096]{1,0:T(8,128)(2,1)} async-done(((bf16[2048,4096]{1,0:T(8,128)(2,1)}), bf16[64,4096]{1,0:T(8,128)(2,1)}) %reduce-scatter.2.cloned.1.call-update) | async-done | bytes 524304 | tf_op jit(solution)/shard_map/reduce_scatter | solution.py:206
  356.4 1.2 fusion.58
  357.6 56.4 %all-reduce.2.cloned.1.call-done = bf16[64,4096]{1,0:T(8,128)(2,1)} async-done(((bf16[64,4096]{1,0:T(8,128)(2,1)}), bf16[64,4096]{1,0:T(8,128)(2,1)}) %all-reduce.2.cloned.1.call-update) | async-done | bytes 524304 | tf_op jit(solution)/shard_map/psum | solution.py:212
  414.0 1.1 convert_multiply_fusion.2
  415.2 0.7 slice.194
  415.9 0.9 slice.193
  (91 shorter events, 18.1 us)
Async XLA Ops:
  7.2 18.6 %copy-start = (s32[32,3]{0,1:T(4,128)S(1)}, s32[32,3]{0,1:T(4,128)}, u32[]{:S(2)}) copy-start(s32[32,3]{0,1:T(4,128)} %param.28) | copy-start | bytes 1156
  7.2 349.2 %reduce-scatter.2.cloned.1.call-start = ((), (), s32[]{:S(2)}) async-start(), calls=%async_computation.1 | async-start | bytes 17301504 | tf_op jit(solution)/shard_map/reduce_scatter | solution.py:206
  8.5 12.7 %copy-start.8 = (bf16[1,128,2048]{2,1,0:T(8,128)(2,1)S(1)}, bf16[1,128,2048]{2,1,0:T(8,128)(2,1)}, u32[]{:S(2)}) copy-start(bf16[1,128,2048]{2,1,0:T(8,128)(2,1)} %param.25) | copy-start | bytes 1572868
  15.2 15.1 %collective-permute-start.1 = (bf16[128,2048]{1,0:T(8,128)(2,1)S(1)}, bf16[128,2048]{1,0:T(8,128)(2,1)S(1)}, u32[]{:S(2)}, u32[]{:S(2)}) collective-permute-start(bf16[128,2048]{1,0:T(8,128)(2,1)S(1)} %slice.186), channel_id=1, source_target_pairs={{1,0},{2,1},{3,2},{4,3},{5,4},{6,5},{7,6},{8,7},{9,8},{10,9},{11,1... | collective-permute-start | bytes 1572872 | tf_op jit(solution)/shard_map/ppermute | solution.py:25
  16.5 14.7 %collective-permute-start = (bf16[128,2048]{1,0:T(8,128)(2,1)S(1)}, bf16[128,2048]{1,0:T(8,128)(2,1)S(1)}, u32[]{:S(2)}, u32[]{:S(2)}) collective-permute-start(bf16[128,2048]{1,0:T(8,128)(2,1)S(1)} %slice.186), channel_id=1, source_target_pairs={{0,1},{1,2},{2,3},{3,4},{4,5},{5,6},{6,7},{7,8},{8,9},{9,10},{10,1... | collective-permute-start | bytes 1572872 | tf_op jit(solution)/shard_map/ppermute | solution.py:24
  21.2 4.0 copy-start.12
  31.6 0.9 copy-start.7
  55.8 2.0 copy-start.5
  55.8 3.4 copy-start.11
  62.5 3.3 copy-start.3
  68.1 1.2 copy-start.4
  72.5 3.2 copy-start.3
  78.1 1.2 copy-start.4
  82.0 2.0 copy-start.6
  82.0 29.3 %copy-start.9 = (bf16[1,128,2048]{2,1,0:T(8,128)(2,1)S(1)}, bf16[1,128,2048]{2,1,0:T(8,128)(2,1)}, u32[]{:S(2)}) copy-start(bf16[1,128,2048]{2,1,0:T(8,128)(2,1)} %param.25) | copy-start | bytes 1572868
  82.0 29.3 %copy-start.10 = (bf16[1,128,8,128]{1,3,2,0:T(8,128)(2,1)S(1)}, bf16[1,128,8,128]{1,3,2,0:T(8,128)(2,1)}, u32[]{:S(2)}) copy-start(bf16[1,128,8,128]{1,3,2,0:T(8,128)(2,1)} %get-tuple-element.747) | copy-start | bytes 786436
  84.0 35.3 %collective-permute-start.2 = (bf16[128,2048]{1,0:T(8,128)(2,1)}, bf16[128,2048]{1,0:T(8,128)(2,1)S(1)}, u32[]{:S(2)}, u32[]{:S(2)}) collective-permute-start(bf16[128,2048]{1,0:T(8,128)(2,1)} %get-tuple-element.754), channel_id=1, source_target_pairs={{1,0},{2,1},{3,2},{4,3},{5,4},{6,5},{7,6},{8,7},{9,8},{10,9},{11,1... | collective-permute-start | bytes 1572872 | tf_op jit(solution)/shard_map/ppermute | solution.py:33
  85.3 35.0 %collective-permute-start.3 = (bf16[128,2048]{1,0:T(8,128)(2,1)}, bf16[128,2048]{1,0:T(8,128)(2,1)S(1)}, u32[]{:S(2)}, u32[]{:S(2)}) collective-permute-start(bf16[128,2048]{1,0:T(8,128)(2,1)} %get-tuple-element.755), channel_id=1, source_target_pairs={{0,1},{1,2},{2,3},{3,4},{4,5},{5,6},{6,7},{7,8},{8,9},{9,10},{10,1... | collective-permute-start | bytes 1572872 | tf_op jit(solution)/shard_map/ppermute | solution.py:33
  111.3 10.5 %copy-start.2 = (bf16[1,128,2048]{2,1,0:T(8,128)(2,1)S(1)}, bf16[1,128,2048]{2,1,0:T(8,128)(2,1)}, u32[]{:S(2)}) copy-start(bf16[1,128,2048]{2,1,0:T(8,128)(2,1)} %param.24) | copy-start | bytes 1572868
  134.9 279.1 %all-reduce.2.cloned.1.call-start = ((), (), s32[]{:S(2)}) async-start(), calls=%async_computation.2 | async-start | bytes 1048576 | tf_op jit(solution)/shard_map/psum | solution.py:212
  356.4 60.4 %copy-start.1 = (s32[32,3]{0,1:T(4,128)S(1)}, s32[32,3]{0,1:T(4,128)}, u32[]{:S(2)}) copy-start(s32[32,3]{0,1:T(4,128)} %param.28) | copy-start | bytes 1156
Sparse Core Ops, SparseCore 0:
  135.1 221.2 reduce-scatter.1
  358.8 55.1 all-reduce.1
where the time goes:
time: 425 us; the launch traced here: 424 us
  waiting for transfers between devices  274 us (64%)
  matrix products  41.1 us (10%)
  starting transfers between devices  33 us (8%)
  local copies, waits for them, and re-layouts  24.2 us (6%)
  other arithmetic  23.4 us (6%)
  between operations  14.4 us (3%)
  loops' own time  13.8 us (3%)
    reduce_scatter x1, waiting for transfers between devices, body(): lax.psum_scatter(jnp.concatenate([term_qkv, term_out], axis=1).astype(jnp...  208 us
    psum x1, waiting for transfers between devices, body(): summed = lax.psum(shares, 'dp').astype(jnp.float32) * factor  56.4 us
    ppermute x2, starting transfers between devices, shifted(): lax.ppermute(value, axis, [(source, source + steps) for source in range(l...  27.1 us
    concatenate x1, other arithmetic, body(): jnp.concatenate([term_qkv, term_out], axis=1).astype(jnp.bfloat16)  9.19 us
    dot_general x1, matrix products, body(): lax.dot_general(grad_qkv, w_qkv, contract_columns, preferred_element_type...  8.9 us
  transfers between devices with their start and end apart: 6, of which 6 were waited for; matrix products, arithmetic and copies ran while one was open for 6% of the time, Pallas kernels for 0%

commit v1 on v0

v1 whole, which is shorter than its diff:
```python
import math

import jax
import jax.numpy as jnp
from jax import lax
from jax.experimental import pallas as pl
from jax.experimental.pallas import tpu as pltpu
from jax.sharding import PartitionSpec as P

LOCAL_HEADS = 8
HEAD = 128
INNER = LOCAL_HEADS * HEAD
D = 2048
TOK_DEV = 128
N_SEQ = 32
RING = 4
GROUP = 2 * RING
QKV_COLS = 3 * INNER // GROUP
OUT_COLS = INNER // GROUP
ROWS = D // N_SEQ
HALF_ROWS = ROWS // 2
LANES = 128
VMEM_LIMIT = 60 * 1024 * 1024

epsilon = 1e-06

BF16 = jnp.bfloat16
F32 = jnp.float32
CONTRACT_COLUMNS = (((1,), (1,)), ((), ()))
CONTRACT_ROWS = (((0,), (0,)), ((), ()))


def place():
    dp, seq = lax.axis_index("dp"), lax.axis_index("seq")
    return seq % 4, (seq // 4) % 4, (seq // 16) * 2 + dp // 2, dp % 2


def at(x, y, z, c):
    return {"dp": (z % 2) * 2 + c, "seq": (z // 2) * 16 + y * 4 + x}


class Copies:
    def __init__(self, send, recv):
        self.send, self.recv, self.used = send, recv, 0

    def start(self, src, dst, device):
        i = self.used
        self.used += 1
        copy = pltpu.make_async_remote_copy(
            src_ref=src,
            dst_ref=dst,
            send_sem=self.send.at[i],
            recv_sem=self.recv.at[i],
            device_id=device,
            device_id_type=pl.DeviceIdType.MESH,
        )
        copy.start()
        return copy


def meet(peers):
    barrier = pltpu.get_barrier_semaphore()
    for peer in peers:
        pl.semaphore_signal(
            barrier, inc=1, device_id=peer, device_id_type=pl.DeviceIdType.MESH
        )
    pl.semaphore_wait(barrier, len(peers))


def lanes(slot, width=LANES):
    return pl.ds(slot * width, width)


def ring_gather(copies, own, out, up, down, partner, local):
    half = out.shape[0] // 2
    low, high = pl.ds(0, half), pl.ds(half, half)
    stay = pltpu.make_async_copy(own, out.at[:, lanes(0)], local)
    stay.start()
    from_down = copies.start(own, out.at[:, lanes(2)], up)
    from_up = copies.start(own, out.at[:, lanes(6)], down)
    rest = [copies.start(own, out.at[:, lanes(1)], partner)]
    yield
    from_down.wait_recv()
    far_low = copies.start(out.at[low, lanes(2)], out.at[low, lanes(4)], up)
    rest.append(copies.start(out.at[:, lanes(2)], out.at[:, lanes(3)], partner))
    yield
    from_up.wait_recv()
    far_high = copies.start(out.at[high, lanes(6)], out.at[high, lanes(4)], down)
    rest.append(copies.start(out.at[:, lanes(6)], out.at[:, lanes(7)], partner))
    yield
    far_low.wait_recv()
    rest.append(copies.start(out.at[low, lanes(4)], out.at[low, lanes(5)], partner))
    yield
    far_high.wait_recv()
    rest.append(copies.start(out.at[high, lanes(4)], out.at[high, lanes(5)], partner))
    yield
    for copy in rest:
        copy.wait()
    for copy in (from_down, from_up, far_low, far_high):
        copy.wait_send()
    stay.wait()


def side_by_side(*steps):
    steps = list(steps)
    while steps:
        for step in list(steps):
            try:
                next(step)
            except StopIteration:
                steps.remove(step)


def gather_kernel(
    normed_t, upstream_t, kv, all_normed, all_upstream, before, after, send, recv, local
):
    x, y, z, c = place()
    dp, seq = lax.axis_index("dp"), lax.axis_index("seq")
    partner = at(x, y, z, 1 - c)
    z_up, z_down = at(x, y, (z + 1) % 4, c), at(x, y, (z + 3) % 4, c)
    y_up, y_down = at(x, (y + 1) % 4, z, c), at(x, (y + 3) % 4, z, c)
    following = {"dp": dp, "seq": (seq + 1) % N_SEQ}
    preceding = {"dp": dp, "seq": (seq + N_SEQ - 1) % N_SEQ}
    meet([partner, z_up, z_down, y_up, y_down, following, preceding])
    copies = Copies(send, recv)
    halo = [copies.start(kv, before, following), copies.start(kv, after, preceding)]
    side_by_side(
        ring_gather(copies, normed_t, all_normed, z_up, z_down, partner, local.at[0]),
        ring_gather(copies, upstream_t, all_upstream, y_up, y_down, partner, local.at[1]),
    )
    for copy in halo:
        copy.wait()


def vmem_specs(count):
    return [pl.BlockSpec(memory_space=pltpu.VMEM)] * count


def communicating(collective_id):
    return pltpu.CompilerParams(
        collective_id=collective_id, has_side_effects=True, vmem_limit_bytes=VMEM_LIMIT
    )


def gather_inputs(normed_t, upstream_t, kv):
    wide = jax.ShapeDtypeStruct((D, GROUP * TOK_DEV), BF16)
    near = jax.ShapeDtypeStruct(kv.shape, BF16)
    return pl.pallas_call(
        gather_kernel,
        out_shape=(wide, wide, near, near),
        in_specs=vmem_specs(3),
        out_specs=tuple(vmem_specs(4)),
        scratch_shapes=[
            pltpu.SemaphoreType.DMA((20,)),
            pltpu.SemaphoreType.DMA((20,)),
            pltpu.SemaphoreType.DMA((2,)),
        ],
        compiler_params=communicating(0),
        name="gather_inputs",
    )(normed_t, upstream_t, kv)


def attention_kernel(
    query, kv, before, after, grad_att, bias, attended, grad_query, own, to_before, to_after
):
    scale = HEAD ** (-0.5)
    for head in range(LOCAL_HEADS):
        cols = pl.ds(head * HEAD, HEAD)
        value_cols = pl.ds(INNER + head * HEAD, HEAD)
        q, grad = query[:, cols], grad_att[:, cols]
        keys = jnp.concatenate([before[:, cols], kv[:, cols], after[:, cols]], axis=0)
        values = jnp.concatenate(
            [before[:, value_cols], kv[:, value_cols], after[:, value_cols]], axis=0
        )
        scores = lax.dot_general(q, keys, CONTRACT_COLUMNS, preferred_element_type=F32)
        scores = scores * scale + bias[0:1, :]
        raised = jnp.exp(scores - jnp.max(scores, axis=1, keepdims=True))
        probability = raised / jnp.sum(raised, axis=1, keepdims=True)
        weights = probability.astype(BF16)
        output = jnp.dot(weights, values, preferred_element_type=F32).astype(BF16)
        attended[:, cols] = output
        delta = jnp.sum(grad.astype(F32) * output.astype(F32), axis=1, keepdims=True)
        grad_prob = lax.dot_general(grad, values, CONTRACT_COLUMNS, preferred_element_type=F32)
        grad_score = (probability * (grad_prob - delta) * scale).astype(BF16)
        grad_query[:, cols] = jnp.dot(grad_score, keys, preferred_element_type=F32).astype(BF16)
        grad_keys = lax.dot_general(grad_score, q, CONTRACT_ROWS, preferred_element_type=F32)
        grad_values = lax.dot_general(weights, grad, CONTRACT_ROWS, preferred_element_type=F32)
        for where, part in ((cols, grad_keys), (value_cols, grad_values)):
            to_before[:, where] = part[:TOK_DEV].astype(BF16)
            own[:, where] = part[TOK_DEV : 2 * TOK_DEV]
            to_after[:, where] = part[2 * TOK_DEV :].astype(BF16)


def attention(query, kv, before, after, grad_att, bias):
    narrow = jax.ShapeDtypeStruct((TOK_DEV, INNER), BF16)
    pair = (TOK_DEV, 2 * INNER)
    return pl.pallas_call(
        attention_kernel,
        out_shape=(
            narrow,
            narrow,
            jax.ShapeDtypeStruct(pair, F32),
            jax.ShapeDtypeStruct(pair, BF16),
            jax.ShapeDtypeStruct(pair, BF16),
        ),
        in_specs=vmem_specs(6),
        out_specs=tuple(vmem_specs(5)),
        compiler_params=pltpu.CompilerParams(vmem_limit_bytes=VMEM_LIMIT),
        name="attention",
    )(query, kv, before, after, grad_att, bias)


def return_kernel(to_before, to_after, from_after, from_before, send, recv):
    dp, seq = lax.axis_index("dp"), lax.axis_index("seq")
    following = {"dp": dp, "seq": (seq + 1) % N_SEQ}
    preceding = {"dp": dp, "seq": (seq + N_SEQ - 1) % N_SEQ}
    meet([following, preceding])
    copies = Copies(send, recv)
    pair = [
        copies.start(to_before, from_after, preceding),
        copies.start(to_after, from_before, following),
    ]
    for copy in pair:
        copy.wait()


def return_halo(to_before, to_after):
    shape = jax.ShapeDtypeStruct(to_before.shape, BF16)
    return pl.pallas_call(
        return_kernel,
        out_shape=(shape, shape),
        in_specs=vmem_specs(2),
        out_specs=tuple(vmem_specs(2)),
        scratch_shapes=[pltpu.SemaphoreType.DMA((2,)), pltpu.SemaphoreType.DMA((2,))],
        compiler_params=communicating(1),
        name="return_halo",
    )(to_before, to_after)


def added(first, *others):
    total = first.astype(F32)
    for other in others:
        total = total + other.astype(F32)
    return total.astype(BF16)


def weight_kernel(
    all_normed,
    all_upstream,
    grad_qkv,
    attended,
    sum_qkv,
    sum_out,
    grads,
    outs,
    part_qkv,
    part_out,
    x_first,
    y_first,
    z_first,
    x_summed,
    y_summed,
    z_summed,
    then_y,
    then_x,
    then_x_out,
    whole_qkv,
    whole_out,
    send,
    recv,
    local,
):
    x, y, z, c = place()
    z_hi, z_lo = z // 2, z % 2
    steps = range(1, RING)

    def in_z(o, other):
        return (z + o) % 4, (c + other) % 2

    def in_y(o, other):
        return (y + o) % 4, (c + other) % 2

    z_group = [(o, other) for o in range(RING) for other in range(2) if o + other]
    finals = [
        (o, lo, other)
        for o in range(RING)
        for lo in range(2)
        for other in range(2)
        if o + lo + other
    ]
    peers = [at((x + o) % 4, y, z, c) for o in steps]
    peers += [at(x, y, (1 - z_hi) * 2 + lo, core) for lo in range(2) for core in range(2)]
    peers += [
        at(x, (y + o) % 4, z_hi * 2 + (z_lo + lo) % 2, (c + other) % 2)
        for o, lo, other in finals
    ]
    meet(peers)
    copies = Copies(send, recv)

    slice_qkv, slice_out = z * 2 + c, y * 2 + c
    stay = [
        pltpu.make_async_copy(
            grad_qkv.at[:, lanes(slice_qkv, QKV_COLS)], grads.at[pl.ds(0, TOK_DEV)], local.at[0]
        ),
        pltpu.make_async_copy(
            attended.at[:, lanes(slice_out, OUT_COLS)], outs.at[pl.ds(0, TOK_DEV)], local.at[1]
        ),
    ]
    for copy in stay:
        copy.start()
    sent_outs, sent_grads = [], []
    for o, other in z_group:
        to, core = in_z(o, other)
        rows = pl.ds((2 * o + other) * TOK_DEV, TOK_DEV)
        sent_grads.append(
            copies.start(
                grad_qkv.at[:, lanes(to * 2 + core, QKV_COLS)], grads.at[rows], at(x, y, to, core)
            )
        )
        to, core = in_y(o, other)
        sent_outs.append(
            copies.start(
                attended.at[:, lanes(to * 2 + core, OUT_COLS)], outs.at[rows], at(x, to, z, core)
            )
        )
    for copy in stay + sent_outs:
        copy.wait()

    def out_chunk(i, carry):
        rows = pl.ds(pl.multiple_of(i * 256, 256), 256)
        product = jnp.dot(all_upstream[rows, :], outs[...], preferred_element_type=F32)
        part_out[i] = product.astype(BF16).reshape(4, ROWS, OUT_COLS)
        return carry

    lax.fori_loop(0, 8, out_chunk, 0)

    def out_part(to):
        return part_out.at[pl.ds((to // 2) * 4, 4), :, pl.ds((to % 2) * HALF_ROWS, HALF_ROWS)]

    z_sent = [
        copies.start(out_part((z + o) % 4), z_first.at[o - 1], at(x, y, (z + o) % 4, c))
        for o in steps
    ]
    for copy in sent_grads:
        copy.wait()

    def qkv_chunk(i, carry):
        rows = pl.ds(pl.multiple_of(i * 256, 256), 256)
        product = jnp.dot(all_normed[rows, :], grads[...], preferred_element_type=F32)
        part_qkv[i] = product.astype(BF16).reshape(4, ROWS, QKV_COLS)
        return carry

    lax.fori_loop(0, 8, qkv_chunk, 0)
    x_sent, y_sent = [], []
    for o in steps:
        to = (x + o) % 4
        x_sent.append(
            copies.start(part_qkv.at[pl.ds(0, 4), to], x_first.at[o - 1], at(to, y, z, c))
        )
        to = (y + o) % 4
        y_sent.append(copies.start(part_qkv.at[4 + to], y_first.at[o - 1], at(x, to, z, c)))

    for copy in z_sent:
        copy.wait()
    z_summed[...] = added(out_part(z)[...], z_first[0], z_first[1], z_first[2])
    out_sent = [
        copies.start(
            z_summed.at[:, (x + o) % 4], then_x_out.at[o - 1], at((x + o) % 4, y, z, c)
        )
        for o in steps
    ]

    for copy in x_sent:
        copy.wait()
    x_summed[...] = added(part_qkv[0:4, x], x_first[0], x_first[1], x_first[2])
    y_then = [
        copies.start(x_summed.at[(y + o) % 4], then_y.at[o - 1], at(x, (y + o) % 4, z, c))
        for o in steps
    ]
    for copy in y_sent:
        copy.wait()
    y_summed[...] = added(part_qkv[4 + y], y_first[0], y_first[1], y_first[2])
    x_then = [
        copies.start(y_summed.at[(x + o) % 4], then_x.at[o - 1], at((x + o) % 4, y, z, c))
        for o in steps
    ]

    for copy in out_sent:
        copy.wait()
    whole_out[...] = added(z_summed[:, x], then_x_out[0], then_x_out[1], then_x_out[2])
    last = []
    out_place = sum_out.at[pl.ds(z_lo * HALF_ROWS, HALF_ROWS), lanes(slice_out, OUT_COLS)]
    for o, lo, other in finals:
        to, core = in_y(o, other)
        last.append(
            copies.start(
                whole_out.at[to], out_place, at(x, to, z_hi * 2 + (z_lo + lo) % 2, core)
            )
        )
    mine = [pltpu.make_async_copy(whole_out.at[y], out_place, local.at[2])]

    for copy in y_then:
        copy.wait()
    whole_qkv[0] = added(x_summed[y], then_y[0], then_y[1], then_y[2])
    for copy in x_then:
        copy.wait()
    whole_qkv[1] = added(y_summed[x], then_x[0], then_x[1], then_x[2])
    qkv_place = sum_qkv.at[:, lanes(slice_qkv, QKV_COLS)]
    for o, other in z_group:
        to, core = in_z(o, other)
        last.append(copies.start(whole_qkv.at[to // 2], qkv_place, at(x, y, to, core)))
    mine.append(pltpu.make_async_copy(whole_qkv.at[z_hi], qkv_place, local.at[3]))
    for copy in mine:
        copy.start()
    for copy in last + mine:
        copy.wait()


def weight_grads(all_normed, all_upstream, grad_qkv, attended):
    tokens = GROUP * TOK_DEV
    scratch = [
        (tokens, QKV_COLS),
        (tokens, OUT_COLS),
        (8, 4, ROWS, QKV_COLS),
        (8, 4, ROWS, OUT_COLS),
        (3, 4, ROWS, QKV_COLS),
        (3, 4, ROWS, QKV_COLS),
        (3, 4, 4, HALF_ROWS, OUT_COLS),
        (4, ROWS, QKV_COLS),
        (4, ROWS, QKV_COLS),
        (4, 4, HALF_ROWS, OUT_COLS),
        (3, ROWS, QKV_COLS),
        (3, ROWS, QKV_COLS),
        (3, 4, HALF_ROWS, OUT_COLS),
        (2, ROWS, QKV_COLS),
        (4, HALF_ROWS, OUT_COLS),
    ]
    return pl.pallas_call(
        weight_kernel,
        out_shape=(
            jax.ShapeDtypeStruct((ROWS, 3 * INNER), BF16),
            jax.ShapeDtypeStruct((ROWS, INNER), BF16),
        ),
        in_specs=vmem_specs(4),
        out_specs=tuple(vmem_specs(2)),
        scratch_shapes=[pltpu.VMEM(shape, BF16) for shape in scratch]
        + [
            pltpu.SemaphoreType.DMA((54,)),
            pltpu.SemaphoreType.DMA((54,)),
            pltpu.SemaphoreType.DMA((4,)),
        ],
        compiler_params=communicating(2),
        name="weight_grads",
    )(all_normed, all_upstream, grad_qkv, attended)


def key_bias(key_blocks, key_count):
    position = lax.axis_index("seq")
    listed = lax.dynamic_index_in_dim(key_blocks, position, 0, keepdims=True)
    used = lax.broadcasted_iota(jnp.int32, listed.shape, 1) < key_count[position]
    block = position - 1 + lax.broadcasted_iota(jnp.int32, (3, 1), 0)
    attended = jnp.any((listed == block) & used, axis=1)
    bias = jnp.where(attended, 0.0, -jnp.inf).astype(F32)
    return jnp.broadcast_to(bias[:, None], (3, TOK_DEV)).reshape(1, 3 * TOK_DEV)


def body(tokens, cotangent, w_qkv, w_out, key_blocks, key_count):
    seq_devices = lax.axis_size("seq")
    factor = 1.0 / math.sqrt(lax.axis_size("dp") * seq_devices * TOK_DEV)
    wide_tokens = tokens[0].astype(F32)
    upstream = cotangent[0]
    inv_rms = lax.rsqrt(jnp.mean(wide_tokens * wide_tokens, axis=1, keepdims=True) + epsilon)
    normed_wide = wide_tokens * inv_rms
    normed = normed_wide.astype(BF16)
    qkv = jnp.dot(normed, w_qkv, preferred_element_type=F32).astype(BF16)
    query, key_value = qkv[:, :INNER], qkv[:, INNER:]
    grad_att = jnp.dot(upstream, w_out, preferred_element_type=F32).astype(BF16)
    all_normed, all_upstream, before, after = gather_inputs(normed.T, upstream.T, key_value)
    attended, grad_query, own, to_before, to_after = attention(
        query, key_value, before, after, grad_att, key_bias(key_blocks, key_count)
    )
    from_after, from_before = return_halo(to_before, to_after)
    grad_kv = own + from_after.astype(F32) + from_before.astype(F32)
    grad_qkv = jnp.concatenate([grad_query, grad_kv.astype(BF16)], axis=1)
    out_proj = lax.dot_general(attended, w_out, CONTRACT_COLUMNS, preferred_element_type=F32)
    layer_out = (wide_tokens + out_proj).astype(BF16)
    grad_normed = lax.dot_general(grad_qkv, w_qkv, CONTRACT_COLUMNS, preferred_element_type=F32)
    branch = inv_rms * (
        grad_normed - normed_wide * jnp.mean(grad_normed * normed_wide, axis=1, keepdims=True)
    )
    grad_tokens = (upstream.astype(F32) + branch).astype(BF16)
    sum_qkv, sum_out = weight_grads(all_normed, all_upstream, grad_qkv, attended)
    return (
        layer_out[None],
        grad_tokens[None],
        sum_qkv.astype(F32) * factor,
        sum_out.astype(F32) * factor,
    )


def solution(mesh):
    return jax.shard_map(
        body,
        mesh=mesh,
        in_specs=(P("dp", "seq", None), P("dp", "seq", None), P(), P(), P(), P()),
        out_specs=(P("dp", "seq", None), P("dp", "seq", None), P("seq", None), P("seq", None)),
        check_vma=False,
    )
```

time: 425 us -> 159 us (0.37)
  waiting for transfers between devices: 274 us -> 0 us
  Pallas kernels: 0 us -> 123 us
  starting transfers between devices: 33 us -> 0 us
  matrix products: 41.1 us -> 20.3 us
  local copies, waits for them, and re-layouts: 24.2 us -> 7.09 us
  other arithmetic: 23.4 us -> 7.25 us
  loops' own time: 13.8 us -> 0 us
  between operations: 14.4 us -> 0.8 us
    reduce_scatter x1 -> x0, waiting for transfers between devices: 208 us -> none  [body(): lax.psum_scatter(jnp.concatenate([term_qkv, term_out], axis=1).astype(jnp...]
    pallas_call x0 -> x4, Pallas kernels: none -> 123 us  [the longest x1 48.2 us: gather_inputs(): pl.pallas_call(gather_kernel, out_shape=(wide, wide, near, near), in_spec...]
    psum x1 -> x0, waiting for transfers between devices: 56.4 us -> none  [body(): summed = lax.psum(shares, 'dp').astype(jnp.float32) * factor]
    ppermute x4 -> x0, starting transfers between devices: 33 us -> none  [the longest x2 27.1 us: shifted(): lax.ppermute(value, axis, [(source, source + steps) for source in range(l...]
    dot_general x20 -> x4, matrix products: 41.1 us -> 20.3 us  [the longest x1 6.5 us: body(): lax.dot_general(grad_qkv, w_qkv, CONTRACT_COLUMNS, preferred_element_type...]
    another operation x3 -> x0, loops' own time: 13.8 us -> none  [the longest x1 4.72 us: attend_backward(): lax.fori_loop(0, total_pairs, back_pass, start_state)]
    ppermute x4 -> x0, waiting for transfers between devices: 9.27 us -> none  [the longest x2 5.79 us: shifted(): lax.ppermute(value, axis, [(source, source + steps) for source in range(l...]
    concatenate x2 -> x1, other arithmetic: 9.3 us -> 0.94 us  [body(): grad_qkv = jnp.concatenate([grad_query, grad_kv.astype(BF16)], axis=1)]
  transfers between devices with their start and end apart: 6 -> 0, of which waited for: 6 -> 0; matrix products, arithmetic and copies ran while one was open for 6% -> 0% of each run, Pallas kernels for 0% -> 0%
where the time goes in v1:
time: 159 us
  Pallas kernels  123 us (77%)
  matrix products  20.3 us (13%)
  other arithmetic  7.25 us (5%)
  local copies, waits for them, and re-layouts  7.09 us (4%)
    pallas_call x1, Pallas kernels, gather_inputs(): pl.pallas_call(gather_kernel, out_shape=(wide, wide, near, near), in_spec...  48.2 us
    pallas_call x1, Pallas kernels, weight_grads(): pl.pallas_call(weight_kernel, out_shape=(jax.ShapeDtypeStruct((ROWS, 3 *...  45.8 us
    pallas_call x1, Pallas kernels, return_halo(): pl.pallas_call(return_kernel, out_shape=(shape, shape), in_specs=vmem_spe...  21.3 us
    pallas_call x1, Pallas kernels, attention(): pl.pallas_call(attention_kernel, out_shape=(narrow, narrow, jax.ShapeDtyp...  8.12 us
    dot_general x1, matrix products, body(): lax.dot_general(grad_qkv, w_qkv, CONTRACT_COLUMNS, preferred_element_type...  6.5 us
    dot_general x1, matrix products, body(): qkv = jnp.dot(normed, w_qkv, preferred_element_type=F32).astype(BF16)  6.41 us
    unnamed x20, local copies, waits for them, and re-layouts  4.03 us
    dot_general x1, matrix products, body(): grad_att = jnp.dot(upstream, w_out, preferred_element_type=F32).astype(BF16)  3.77 us

profile of v1, /device:TPU:1, one launch (start us, length us, event | category | flops | bytes accessed | tf_op | source)
XLA Modules:
  0.0 158.9 jit_solution(9072472495679148689)
XLA Ops:
  0.6 0.0 copy-start
  0.6 0.0 copy-start.2
  0.7 0.0 copy-start.5
  0.7 1.3 dynamic_slice.8
  2.0 0.6 iota_compare_fusion
  2.7 0.0 copy-done
  2.7 0.2 dynamic-slice_reduce_fusion
  2.9 0.2 and_reduce_fusion
  3.1 0.1 broadcast_bitcast_fusion
  3.1 0.6 copy.28
  3.7 3.8 %convolution_convert_fusion.1.grad_att = bf16[128,1024]{1,0:T(8,128)(2,1)} fusion(bf16[2048,1024]{1,0:T(8,128)(2,1)} %param.9, bf16[1,128,2048]{2,1,0:T(8,128)(2,1)} %param.7), kind=kOutput, calls=%fused_computation.9 | convolution fusion | flops 537001984 | bytes 4980736 | tf_op jit(solution)/shard_map/dot_general | solution.py:477
  7.5 0.0 copy-done.5
  7.5 0.3 copy.17
  7.8 0.3 fusion.10
  8.1 0.0 copy-done.2
  8.1 1.0 copy.18
  9.1 0.9 fusion.13.normed_t
  10.0 6.4 %convolution_convert_fusion = bf16[128,3072]{1,0:T(8,128)(2,1)S(1)} fusion(bf16[2048,3072]{1,0:T(8,128)(2,1)} %param.8, bf16[1,128,2048]{1,2,0:T(8,128)(2,1)S(1)} %copy.17, f32[128]{0:T(128)S(1)} %add_rsqrt_fusion), kind=kOutput, calls=%fused_computation | convolution fusion | flops 1611792384 | bytes 13894144 | tf_op jit(solution)/shard_map/dot_general | solution.py:475
  16.4 0.7 slice.8.query
  17.1 0.8 slice.9.kv
  17.9 48.2 %gather_inputs.1 = (bf16[2048,1024]{1,0:T(8,128)(2,1)}, bf16[2048,1024]{1,0:T(8,128)(2,1)}, bf16[128,2048]{1,0:T(8,128)(2,1)}, bf16[128,2048]{1,0:T(8,128)(2,1)}) custom-call(bf16[2048,128]{1,0:T(8,128)(2,1)} %fusion.13.normed_t, bf16[2048,128]{1,0:T(8,128)(2,1)} %bitcast.35, bf16[128,2048]{1,0:T(8,128)(2,1)} %slice.9.kv), custom_call_target="tpu_custom_call" | custom-call | tf_op jit(solution)/shard_map/gather_inputs/pallas_call | solution.py:148
  66.2 8.1 %attention.1 = (bf16[128,1024]{1,0:T(8,128)(2,1)}, bf16[128,1024]{1,0:T(8,128)(2,1)}, f32[128,2048]{1,0:T(8,128)}, bf16[128,2048]{1,0:T(8,128)(2,1)}, bf16[128,2048]{1,0:T(8,128)(2,1)}) custom-call(bf16[128,1024]{1,0:T(8,128)(2,1)} %slice.8.query, bf16[128,2048]{1,0:T(8,128)(2,1)} %slice.9.kv, bf16[128,2048]{1,0:T(8,128)(2,1)} %get-tuple-element.17.before, ...), custom_call_target="tpu_custom_call" | custom-call | tf_op jit(solution)/shard_map/attention/pallas_call | solution.py:197
  74.3 0.0 copy-start.4
  74.3 3.6 %fusion.1 = bf16[1,128,2048]{1,2,0:T(8,128)(2,1)S(1)} fusion(bf16[128,1024]{1,0:T(8,128)(2,1)} %get-tuple-element.19.attended, bf16[2048,1024]{1,0:T(8,128)(2,1)} %param.9, bf16[1,128,2048]{1,2,0:T(8,128)(2,1)S(1)} %copy.17), kind=kOutput, calls=%fused_computation.3 | convolution fusion | flops 537657344 | bytes 5505024 | tf_op jit(solution)/shard_map/dot_general | solution.py:485
  77.9 0.0 copy-start.3
  77.9 1.0 copy.22
  79.0 21.3 %return_halo.1 = (bf16[128,2048]{1,0:T(8,128)(2,1)}, bf16[128,2048]{1,0:T(8,128)(2,1)}) custom-call(bf16[128,2048]{1,0:T(8,128)(2,1)} %get-tuple-element.22.to_before, bf16[128,2048]{1,0:T(8,128)(2,1)} %get-tuple-element.23.to_after), custom_call_target="tpu_custom_call" | custom-call | tf_op jit(solution)/shard_map/return_halo/pallas_call | solution.py:229
  100.3 0.0 copy-done.4
  100.3 1.4 add_convert_fusion
  101.7 0.0 copy-done.3
  101.8 0.9 pad_maximum_fusion.grad_qkv
  102.7 45.8 %weight_grads.1 = (bf16[64,3072]{1,0:T(8,128)(2,1)}, bf16[64,1024]{1,0:T(8,128)(2,1)}) custom-call(bf16[2048,1024]{1,0:T(8,128)(2,1)} %get-tuple-element.26.all_normed, bf16[2048,1024]{1,0:T(8,128)(2,1)} %get-tuple-element.27.all_upstream, bf16[128,3072]{1,0:T(8,128)(2,1)} %pad_maximum_fusion.grad_qkv, bf16[128,1024]{1,0:T(8,128)(2,1)} %get-tuple-element.19.attended), custom_call_target="tpu_custom_call" | custom-call | tf_op jit(solution)/shard_map/weight_grads/pallas_call | solution.py:438
  148.5 1.6 %convert_multiply_fusion.3 = f32[64,1024]{1,0:T(8,128)} fusion(bf16[64,1024]{1,0:T(8,128)(2,1)} %get-tuple-element.29), kind=kLoop, calls=%fused_computation.22 | loop fusion | flops 131072 | bytes 393216 | tf_op jit(solution)/shard_map/mul | solution.py:497
  150.2 0.0 copy-start.1
  150.2 0.0 copy-start.6
  150.2 6.5 %fusion.5 = (f32[128]{0:T(128)S(1)}, f32[128,2048]{0,1:T(8,128)S(1)}) fusion(bf16[1,128,2048]{1,2,0:T(8,128)(2,1)S(1)} %copy.17, f32[128]{0:T(128)S(1)} %add_rsqrt_fusion, bf16[2048,3072]{1,0:T(8,128)(2,1)} %param.8, bf16[128,2048]{1,0:T(8,128)(2,1)S(1)} %add_convert_fusion, bf16[128,1024]{1,0:T(8,128)(2,1)S(1)} %copy-done.3), kind=kOutput, calls=%fused_computation.10 | convolution fusion | flops 1613234048 | bytes 14943232 | tf_op jit(solution)/shard_map/dot_general | solution.py:487
  156.7 0.0 copy-done.1
  156.7 0.3 fusion.11
  157.0 1.0 copy.23
  158.0 0.0 copy-done.6
  158.0 0.9 convert_multiply_fusion.2
  (4 shorter events, 0.0 us)
Async XLA Ops:
  0.6 2.0 %copy-start = (s32[32,3]{0,1:T(4,128)S(1)}, s32[32,3]{0,1:T(4,128)}, u32[]{:S(2)}) copy-start(s32[32,3]{0,1:T(4,128)} %param.10) | copy-start | bytes 1156
  0.6 7.4 %copy-start.2 = (bf16[1,128,2048]{2,1,0:T(8,128)(2,1)S(1)}, bf16[1,128,2048]{2,1,0:T(8,128)(2,1)}, u32[]{:S(2)}) copy-start(bf16[1,128,2048]{2,1,0:T(8,128)(2,1)} %param.7) | copy-start | bytes 1572868
  0.7 6.8 %copy-start.5 = (bf16[1,128,2048]{2,1,0:T(8,128)(2,1)S(1)}, bf16[1,128,2048]{2,1,0:T(8,128)(2,1)}, u32[]{:S(2)}) copy-start(bf16[1,128,2048]{2,1,0:T(8,128)(2,1)} %param.6) | copy-start | bytes 1572868
  74.3 26.0 %copy-start.4 = (f32[128,2048]{1,0:T(8,128)S(1)}, f32[128,2048]{1,0:T(8,128)}, u32[]{:S(2)}) copy-start(f32[128,2048]{1,0:T(8,128)} %get-tuple-element.21) | copy-start | bytes 3145732
  77.9 23.8 %copy-start.3 = (bf16[128,1024]{1,0:T(8,128)(2,1)S(1)}, bf16[128,1024]{1,0:T(8,128)(2,1)}, u32[]{:S(2)}) copy-start(bf16[128,1024]{1,0:T(8,128)(2,1)} %get-tuple-element.20) | copy-start | bytes 786436
  150.2 6.5 %copy-start.1 = (bf16[1,128,2048]{1,2,0:T(8,128)(2,1)S(1)}, bf16[1,128,2048]{1,2,0:T(8,128)(2,1)}, u32[]{:S(2)}) copy-start(bf16[1,128,2048]{1,2,0:T(8,128)(2,1)} %copy.18) | copy-start | bytes 1572868
  150.2 7.8 %copy-start.6 = (bf16[64,3072]{1,0:T(8,128)(2,1)S(1)}, bf16[64,3072]{1,0:T(8,128)(2,1)}, u32[]{:S(2)}) copy-start(bf16[64,3072]{1,0:T(8,128)(2,1)} %get-tuple-element.28) | copy-start | bytes 1179652

commit v2 on v0

v2 whole, which is shorter than its diff:
```python
import functools
import math

import jax
import jax.numpy as jnp
from jax import lax
from jax.experimental import pallas as pl
from jax.experimental.pallas import tpu as pltpu
from jax.sharding import PartitionSpec as P

LOCAL_HEADS = 8
HEAD = 128
INNER = LOCAL_HEADS * HEAD
D = 2048
TOK_DEV = 128
N_SEQ = 32
RING = 4
GROUP = 2 * RING
WINDOW = 3 * TOK_DEV
ALL_TOK = GROUP * TOK_DEV
ROWS = D // N_SEQ
WIDE = 256
VMEM_LIMIT = 63 * 1024 * 1024

epsilon = 1e-06

BF16 = jnp.bfloat16
F32 = jnp.float32
CONTRACT_COLUMNS = (((1,), (1,)), ((), ()))
CONTRACT_ROWS = (((0,), (0,)), ((), ()))
STEPS = range(1, RING)
Z_GROUP = [(o, other) for o in range(RING) for other in range(2) if o + other]


def place():
    dp, seq = lax.axis_index("dp"), lax.axis_index("seq")
    return seq % 4, (seq // 4) % 4, (seq // 16) * 2 + dp // 2, dp % 2


def at(x, y, z, c):
    return {"dp": (z % 2) * 2 + c, "seq": (z // 2) * 16 + y * 4 + x}


def lanes(slot, width=HEAD):
    start = slot * width
    return pl.ds(start if isinstance(start, int) else pl.multiple_of(start, width), width)


def remote(src, dst, send, recv, device):
    return pltpu.make_async_remote_copy(
        src_ref=src,
        dst_ref=dst,
        send_sem=send,
        recv_sem=recv,
        device_id=device,
        device_id_type=pl.DeviceIdType.MESH,
    )


class Copies:
    def __init__(self, send, recv):
        self.send, self.recv, self.used = send, recv, 0

    def reserve(self, count):
        first = self.used
        self.used += count
        return first

    def start(self, src, dst, device):
        i = self.reserve(1)
        copy = remote(src, dst, self.send.at[i], self.recv.at[i], device)
        copy.start()
        return copy


def wait_all(copies):
    for copy in copies:
        copy.wait()


def signal_all(peers):
    barrier = pltpu.get_barrier_semaphore()
    for peer in peers:
        pl.semaphore_signal(
            barrier, inc=1, device_id=peer, device_id_type=pl.DeviceIdType.MESH
        )


def ring_gather(copies, view, up, down, partner):
    from_down = copies.start(view(0, None), view(2, None), up)
    from_up = copies.start(view(0, None), view(6, None), down)
    rest = [copies.start(view(0, None), view(1, None), partner)]
    yield
    from_down.wait_recv()
    far_low = copies.start(view(2, 0), view(4, 0), up)
    from_up.wait_recv()
    far_high = copies.start(view(6, 1), view(4, 1), down)
    rest.append(copies.start(view(2, None), view(3, None), partner))
    rest.append(copies.start(view(6, None), view(7, None), partner))
    yield
    far_low.wait_recv()
    rest.append(copies.start(view(4, 0), view(5, 0), partner))
    far_high.wait_recv()
    rest.append(copies.start(view(4, 1), view(5, 1), partner))
    yield
    wait_all(rest)
    for copy in (from_down, from_up, far_low, far_high):
        copy.wait_send()
    yield


def added(first, *others):
    total = first.astype(F32)
    for other in others:
        total = total + other.astype(F32)
    return total.astype(BF16)


def layer_kernel(
    tokens_hbm,
    upstream_hbm,
    w_qkv_hbm,
    w_out_hbm,
    key_blocks,
    key_count,
    layer_out,
    grad_tokens,
    sum_a,
    sum_b,
    sum_out,
    tokens,
    upstream,
    w_query,
    w_keys,
    w_values,
    w_out,
    inv_rms,
    normed,
    upstream_t,
    all_normed,
    cot_rows,
    all_attended,
    query,
    kv,
    before,
    after,
    grad_att,
    probability,
    attended,
    grad_query,
    grad_keys,
    grad_values,
    own,
    to_before,
    to_after,
    from_after,
    from_before,
    grad_normed,
    grads_a,
    grads_b,
    part_a,
    part_b,
    part_out,
    x_first_a,
    y_first_a,
    x_first_b,
    y_first_b,
    y_first_out,
    x_summed_a,
    y_summed_a,
    x_summed_b,
    y_summed_b,
    y_summed_out,
    then_y_a,
    then_x_a,
    then_y_b,
    then_x_b,
    then_x_out,
    whole_a,
    whole_b,
    whole_out,
    send,
    recv,
    local,
):
    x, y, z, c = place()
    dp, seq = lax.axis_index("dp"), lax.axis_index("seq")
    z_hi, z_lo = z // 2, z % 2
    mine = z * 2 + c
    following = {"dp": dp, "seq": (seq + 1) % N_SEQ}
    preceding = {"dp": dp, "seq": (seq + N_SEQ - 1) % N_SEQ}
    has_after, has_before = seq < N_SEQ - 1, seq > 0
    scale = HEAD ** (-0.5)
    copies = Copies(send, recv)

    loads = {}
    for i, (name, src, dst) in enumerate(
        [
            ("tokens", tokens_hbm, tokens),
            ("keys", w_qkv_hbm.at[:, pl.ds(INNER, INNER)], w_keys),
            ("values", w_qkv_hbm.at[:, pl.ds(2 * INNER, INNER)], w_values),
            ("upstream", upstream_hbm, upstream),
            ("query", w_qkv_hbm.at[:, pl.ds(0, INNER)], w_query),
            ("out", w_out_hbm, w_out),
        ]
    ):
        loads[name] = pltpu.make_async_copy(src, dst, local.at[i])
        loads[name].start()

    peers = [
        at(x, (y + o) % 4, z_hi * 2 + (z_lo + lo) % 2, (c + other) % 2)
        for o in range(RING)
        for lo in range(2)
        for other in range(2)
        if o + lo + other
    ]
    peers += [at(x, y, (1 - z_hi) * 2 + lo, core) for lo in range(2) for core in range(2)]
    peers += [at((x + o) % 4, y, z, c) for o in STEPS]
    peers += [following, preceding]
    signal_all(peers)

    zero_block = jnp.zeros((TOK_DEV, 2 * INNER), BF16)

    @pl.when(jnp.logical_not(has_before))
    def _():
        before[...] = zero_block
        from_before[...] = zero_block

    @pl.when(jnp.logical_not(has_after))
    def _():
        after[...] = zero_block
        from_after[...] = zero_block

    count = key_count[seq]
    listed = [key_blocks[seq * 3 + j] for j in range(3)]
    biases = []
    for shift in (-1, 0, 1):
        used = jnp.int32(0)
        for j in range(3):
            hit = jnp.where(listed[j] == seq + shift, 1, 0) * jnp.where(j < count, 1, 0)
            used = used + hit
        used = jnp.full((1, TOK_DEV), used, jnp.int32)
        biases.append(jnp.where(used > 0, 0.0, -jnp.inf).astype(F32))
    bias = jnp.concatenate(biases, axis=1)

    loads["tokens"].wait()
    wide_tokens = tokens[...].astype(F32)
    inv_rms[...] = lax.rsqrt(jnp.mean(wide_tokens * wide_tokens, axis=1, keepdims=True) + epsilon)
    normed[...] = (wide_tokens * inv_rms[...]).astype(BF16)

    def project(rows, weight, out, first):
        def chunk(i, carry):
            product = jnp.dot(rows[...], weight[:, lanes(i, WIDE)], preferred_element_type=F32)
            out[:, lanes(i + first, WIDE)] = product.astype(BF16)
            return carry

        lax.fori_loop(0, INNER // WIDE, chunk, 0)

    def halo(i, part):
        cols = pl.ds(part * INNER, INNER)
        return (
            remote(kv.at[:, cols], before.at[:, cols], send.at[i], recv.at[i], following),
            remote(kv.at[:, cols], after.at[:, cols], send.at[i + 1], recv.at[i + 1], preceding),
        )

    halo_at = [copies.reserve(2), copies.reserve(2)]

    def send_halo(part):
        forth, back = halo(halo_at[part], part)

        @pl.when(has_after)
        def _():
            forth.start()

        @pl.when(has_before)
        def _():
            back.start()

    def take_halo(part):
        forth, back = halo(halo_at[part], part)

        @pl.when(has_after)
        def _():
            forth.wait_send()
            back.wait_recv()

        @pl.when(has_before)
        def _():
            back.wait_send()
            forth.wait_recv()

    loads["keys"].wait()
    project(normed, w_keys, kv, 0)
    pl.semaphore_wait(pltpu.get_barrier_semaphore(), len(peers))
    send_halo(0)
    loads["values"].wait()
    project(normed, w_values, kv, INNER // WIDE)
    send_halo(1)

    def turn(rows, out):
        def chunk(i, carry):
            out[pl.ds(pl.multiple_of(i * WIDE, WIDE), WIDE), pl.ds(0, TOK_DEV)] = jnp.transpose(
                rows[:, lanes(i, WIDE)]
            )
            return carry

        lax.fori_loop(0, D // WIDE, chunk, 0)

    partner = at(x, y, z, 1 - c)
    z_up, z_down = at(x, y, (z + 1) % 4, c), at(x, y, (z + 3) % 4, c)

    def in_z(o, other):
        return (z + o) % 4, (c + other) % 2

    def normed_view(slot, part):
        rows = pl.ds(0, D) if part is None else pl.ds(part * (D // 2), D // 2)
        return all_normed.at[rows, lanes(slot)]

    def attended_view(slot, part):
        cols = pl.ds(0, INNER) if part is None else pl.ds(part * (INNER // 2), INNER // 2)
        return all_attended.at[lanes(slot), cols]

    def exchange(src_view, dst_view):
        sent = []
        for o, other in Z_GROUP:
            to, core = in_z(o, other)
            sent.append(
                copies.start(src_view(to * 2 + core), dst_view(2 * o + other), at(x, y, to, core))
            )
        return sent

    turn(normed, all_normed)
    normed_ring = ring_gather(copies, normed_view, z_up, z_down, partner)
    next(normed_ring)
    loads["upstream"].wait()
    turn(upstream, upstream_t)

    def turned(index):
        return upstream_t.at[pl.ds(pl.multiple_of(index * WIDE, WIDE), WIDE), :]

    keep = [pltpu.make_async_copy(turned(mine), cot_rows.at[:, lanes(0)], local.at[6])]
    keep[0].start()
    sent_cot = exchange(turned, lambda slot: cot_rows.at[:, lanes(slot)])
    loads["query"].wait()
    project(normed, w_query, query, 0)
    loads["out"].wait()
    project(upstream, w_out, grad_att, 0)

    def pairs(body):
        def step(i, carry):
            for head in (2 * i, 2 * i + 1):
                body(head)
            return carry

        return step

    def window(cols):
        return jnp.concatenate([before[:, cols], kv[:, cols], after[:, cols]], axis=0)

    def value_cols(head):
        return lanes(head + LOCAL_HEADS)

    def weigh(head):
        cols = lanes(head)
        scores = lax.dot_general(
            query[:, cols], window(cols), CONTRACT_COLUMNS, preferred_element_type=F32
        )
        scores = scores * scale + bias
        raised = jnp.exp(scores - jnp.max(scores, axis=1, keepdims=True))
        probability[head] = raised / jnp.sum(raised, axis=1, keepdims=True)

    def give_back(part, cols):
        to_before[:, cols] = part[:TOK_DEV].astype(BF16)
        own[:, cols] = part[TOK_DEV : 2 * TOK_DEV]
        to_after[:, cols] = part[2 * TOK_DEV :].astype(BF16)

    def attend(head):
        cols = lanes(head)
        weights = probability[head].astype(BF16)
        output = jnp.dot(weights, window(value_cols(head)), preferred_element_type=F32)
        attended[:, cols] = output.astype(BF16)
        part = lax.dot_general(
            weights, grad_att[:, cols], CONTRACT_ROWS, preferred_element_type=F32
        )
        give_back(part, value_cols(head))

    def attend_back(head):
        cols = lanes(head)
        grad = grad_att[:, cols]
        keys = window(cols)
        delta = jnp.sum(
            grad.astype(F32) * attended[:, cols].astype(F32), axis=1, keepdims=True
        )
        grad_prob = lax.dot_general(
            grad, window(value_cols(head)), CONTRACT_COLUMNS, preferred_element_type=F32
        )
        grad_score = (probability[head] * (grad_prob - delta) * scale).astype(BF16)
        grad_query[:, cols] = jnp.dot(grad_score, keys, preferred_element_type=F32).astype(BF16)
        part = lax.dot_general(
            grad_score, query[:, cols], CONTRACT_ROWS, preferred_element_type=F32
        )
        give_back(part, cols)

    pair_count = LOCAL_HEADS // 2
    back_at = copies.reserve(4 * pair_count)

    def returned(i):
        cols = lanes(i, 2 * HEAD)
        down, up = back_at + i, back_at + 2 * pair_count + i
        return (
            remote(
                to_before.at[:, cols], from_after.at[:, cols], send.at[down], recv.at[down], preceding
            ),
            remote(
                to_after.at[:, cols], from_before.at[:, cols], send.at[up], recv.at[up], following
            ),
        )

    def send_back(i):
        down, up = returned(i)

        @pl.when(has_before)
        def _():
            down.start()

        @pl.when(has_after)
        def _():
            up.start()

    def take_back(first):
        @pl.when(has_after)
        def _():
            for i in range(first, first + pair_count):
                down, up = returned(i)
                down.wait_recv()
                up.wait_send()

        @pl.when(has_before)
        def _():
            for i in range(first, first + pair_count):
                down, up = returned(i)
                down.wait_send()
                up.wait_recv()

    def settle(out, first):
        cols = pl.ds(first, INNER)
        out[...] = added(own[:, cols], from_after[:, cols], from_before[:, cols])

    take_halo(0)
    lax.fori_loop(0, pair_count, pairs(weigh), 0)
    take_halo(1)

    def attend_pair(i, carry):
        pairs(attend)(i, carry)
        send_back(i + pair_count)
        return carry

    lax.fori_loop(0, pair_count, attend_pair, 0)
    all_attended[pl.ds(0, TOK_DEV), :] = attended[...]
    next(normed_ring)
    attended_ring = ring_gather(copies, attended_view, z_up, z_down, partner)
    next(attended_ring)

    def back_pair(i, carry):
        pairs(attend_back)(i, carry)
        send_back(i)
        return carry

    lax.fori_loop(0, pair_count, back_pair, 0)

    def swap_columns(src, dst, cols, i):
        stay = pltpu.make_async_copy(
            src.at[:, lanes(mine)], dst.at[pl.ds(0, TOK_DEV), cols], local.at[i]
        )
        stay.start()
        return [stay] + exchange(
            lambda index: src.at[:, lanes(index)], lambda slot: dst.at[lanes(slot), cols]
        )

    sent_query = swap_columns(grad_query, grads_a, pl.ds(0, HEAD), 7)

    def out_chunk(i, carry):
        cols = lanes(i, WIDE)
        rows = pl.ds(pl.multiple_of(i * WIDE, WIDE), WIDE)
        product = lax.dot_general(
            attended[...], w_out[rows, :], CONTRACT_COLUMNS, preferred_element_type=F32
        )
        layer_out[:, cols] = (tokens[:, cols].astype(F32) + product).astype(BF16)
        return carry

    lax.fori_loop(0, D // WIDE, out_chunk, 0)
    next(normed_ring)
    next(attended_ring)

    take_back(pair_count)
    settle(grad_values, INNER)
    sent_values = swap_columns(grad_values, grads_a, pl.ds(HEAD, HEAD), 8)

    def grad_chunk_a(i, carry):
        rows = pl.ds(pl.multiple_of(i * WIDE, WIDE), WIDE)
        grad_normed[:, lanes(i, WIDE)] = lax.dot_general(
            grad_query[...], w_query[rows, :], CONTRACT_COLUMNS, preferred_element_type=F32
        ) + lax.dot_general(
            grad_values[...], w_values[rows, :], CONTRACT_COLUMNS, preferred_element_type=F32
        )
        return carry

    lax.fori_loop(0, D // WIDE, grad_chunk_a, 0)
    take_back(0)
    settle(grad_keys, 0)
    sent_keys = swap_columns(grad_keys, grads_b, pl.ds(0, HEAD), 9)
    next(normed_ring)
    next(attended_ring)

    def multiply(grads, part, width, first):
        def chunk(i, carry):
            rows = pl.ds(pl.multiple_of(i * WIDE, WIDE), WIDE)
            product = jnp.dot(all_normed[rows, :], grads[...], preferred_element_type=F32)
            part[i] = product.astype(BF16).reshape(4, ROWS, width)
            return carry

        lax.fori_loop(first, first + 4, chunk, 0)

    def scatter(grads, part, width, x_first, y_first):
        multiply(grads, part, width, 0)
        x_sent = [
            copies.start(
                part.at[pl.ds(0, 4), (x + o) % 4], x_first.at[o - 1], at((x + o) % 4, y, z, c)
            )
            for o in STEPS
        ]
        multiply(grads, part, width, 4)
        y_sent = [
            copies.start(part.at[4 + (y + o) % 4], y_first.at[o - 1], at(x, (y + o) % 4, z, c))
            for o in STEPS
        ]
        return x_sent, y_sent

    def scatter_on(sent, part, x_first, y_first, x_summed, y_summed, then_y, then_x):
        x_sent, y_sent = sent
        wait_all(x_sent)
        x_summed[...] = added(part[0:4, x], x_first[0], x_first[1], x_first[2])
        y_then = [
            copies.start(x_summed.at[(y + o) % 4], then_y.at[o - 1], at(x, (y + o) % 4, z, c))
            for o in STEPS
        ]
        wait_all(y_sent)
        y_summed[...] = added(part[4 + y], y_first[0], y_first[1], y_first[2])
        x_then = [
            copies.start(y_summed.at[(x + o) % 4], then_x.at[o - 1], at((x + o) % 4, y, z, c))
            for o in STEPS
        ]
        return y_then, x_then

    def gather_sums(sent, x_summed, y_summed, then_y, then_x, whole, out, width, i):
        y_then, x_then = sent
        wait_all(y_then)
        whole[0] = added(x_summed[y], then_y[0], then_y[1], then_y[2])
        wait_all(x_then)
        whole[1] = added(y_summed[x], then_x[0], then_x[1], then_x[2])
        own_place = out.at[:, lanes(mine, width)]
        stay = pltpu.make_async_copy(whole.at[z_hi], own_place, local.at[i])
        stay.start()
        last = [stay]
        for o, other in Z_GROUP:
            to, core = in_z(o, other)
            last.append(copies.start(whole.at[to // 2], own_place, at(x, y, to, core)))
        return last

    wait_all(sent_query + sent_values)
    sent_a = scatter(grads_a, part_a, 2 * HEAD, x_first_a, y_first_a)

    wait_all(keep + sent_cot)
    next(attended_ring)

    def out_part(i, carry):
        cols = lanes(i, WIDE)
        product = jnp.dot(cot_rows[...], all_attended[:, cols], preferred_element_type=F32)
        part_out[:, :, cols] = product.astype(BF16).reshape(4, ROWS, WIDE)
        return carry

    lax.fori_loop(0, INNER // WIDE, out_part, 0)
    y_sent_out = [
        copies.start(
            part_out.at[:, :, lanes((y + o) % 4, WIDE)],
            y_first_out.at[o - 1],
            at(x, (y + o) % 4, z, c),
        )
        for o in STEPS
    ]

    wait_all(sent_keys)
    sent_b = scatter(grads_b, part_b, HEAD, x_first_b, y_first_b)

    def grad_chunk_b(i, total):
        rows, cols = pl.ds(pl.multiple_of(i * WIDE, WIDE), WIDE), lanes(i, WIDE)
        product = grad_normed[:, cols] + lax.dot_general(
            grad_keys[...], w_keys[rows, :], CONTRACT_COLUMNS, preferred_element_type=F32
        )
        grad_normed[:, cols] = product
        along = product * (tokens[:, cols].astype(F32) * inv_rms[...])
        return total + jnp.sum(along, axis=1, keepdims=True)

    total = lax.fori_loop(0, D // WIDE, grad_chunk_b, jnp.zeros((TOK_DEV, 1), F32))
    mean = total * (1.0 / D)

    def tokens_chunk(i, carry):
        cols = lanes(i, WIDE)
        normed_wide = tokens[:, cols].astype(F32) * inv_rms[...]
        branch = inv_rms[...] * (grad_normed[:, cols] - normed_wide * mean)
        grad_tokens[:, cols] = (upstream[:, cols].astype(F32) + branch).astype(BF16)
        return carry

    then_a = scatter_on(
        sent_a, part_a, x_first_a, y_first_a, x_summed_a, y_summed_a, then_y_a, then_x_a
    )
    wait_all(y_sent_out)
    y_summed_out[...] = added(
        part_out[:, :, lanes(y, WIDE)], y_first_out[0], y_first_out[1], y_first_out[2]
    )
    x_then_out = [
        copies.start(
            y_summed_out.at[(x + o) % 4], then_x_out.at[o - 1], at((x + o) % 4, y, z, c)
        )
        for o in STEPS
    ]
    lax.fori_loop(0, D // WIDE, tokens_chunk, 0)
    then_b = scatter_on(
        sent_b, part_b, x_first_b, y_first_b, x_summed_b, y_summed_b, then_y_b, then_x_b
    )
    last = gather_sums(
        then_a, x_summed_a, y_summed_a, then_y_a, then_x_a, whole_a, sum_a, 2 * HEAD, 10
    )

    wait_all(x_then_out)
    whole_out[...] = added(y_summed_out[x], then_x_out[0], then_x_out[1], then_x_out[2])
    final_at = copies.reserve(4)
    owner = 2 * z_lo + c
    holds_own = y == owner
    out_place = sum_out.at[:, lanes(y, WIDE)]
    outgoing = [
        remote(
            whole_out,
            out_place,
            send.at[final_at + 2 * lo + other],
            recv.at[final_at + y],
            at(x, owner, z_hi * 2 + (z_lo + lo) % 2, (c + other) % 2),
        )
        for lo in range(2)
        for other in range(2)
    ]
    for copy in outgoing[1:]:
        copy.start()

    @pl.when(jnp.logical_not(holds_own))
    def _():
        outgoing[0].start()

    @pl.when(holds_own)
    def _():
        stay = pltpu.make_async_copy(whole_out, out_place, local.at[12])
        stay.start()
        stay.wait()

    last += gather_sums(
        then_b, x_summed_b, y_summed_b, then_y_b, then_x_b, whole_b, sum_b, HEAD, 11
    )
    for copy in outgoing[1:]:
        copy.wait_send()

    @pl.when(jnp.logical_not(holds_own))
    def _():
        outgoing[0].wait_send()

    for source in range(RING):
        incoming = remote(
            whole_out,
            sum_out.at[:, lanes(source, WIDE)],
            send.at[final_at],
            recv.at[final_at + source],
            at(x, source, z_hi * 2 + y // 2, y % 2),
        )

        @pl.when(jnp.logical_not(holds_own & (y == source)))
        def _(incoming=incoming):
            incoming.wait_recv()

    wait_all(last)


def whole_layer(tokens, upstream, w_qkv, w_out, key_blocks, key_count):
    pair = (TOK_DEV, 2 * INNER)
    narrow = (TOK_DEV, INNER)
    full = (TOK_DEV, D)
    weight = (D, INNER)
    scratch = [
        (full, BF16),
        (full, BF16),
        (weight, BF16),
        (weight, BF16),
        (weight, BF16),
        (weight, BF16),
        ((TOK_DEV, 1), F32),
        (full, BF16),
        ((D, TOK_DEV), BF16),
        ((D, ALL_TOK), BF16),
        ((WIDE, ALL_TOK), BF16),
        ((ALL_TOK, INNER), BF16),
        (narrow, BF16),
        (pair, BF16),
        (pair, BF16),
        (pair, BF16),
        (narrow, BF16),
        ((LOCAL_HEADS, TOK_DEV, WINDOW), F32),
        (narrow, BF16),
        (narrow, BF16),
        (narrow, BF16),
        (narrow, BF16),
        (pair, F32),
        (pair, BF16),
        (pair, BF16),
        (pair, BF16),
        (pair, BF16),
        (full, F32),
        ((ALL_TOK, 2 * HEAD), BF16),
        ((ALL_TOK, HEAD), BF16),
        ((8, 4, ROWS, 2 * HEAD), BF16),
        ((8, 4, ROWS, HEAD), BF16),
        ((4, ROWS, INNER), BF16),
        ((3, 4, ROWS, 2 * HEAD), BF16),
        ((3, 4, ROWS, 2 * HEAD), BF16),
        ((3, 4, ROWS, HEAD), BF16),
        ((3, 4, ROWS, HEAD), BF16),
        ((3, 4, ROWS, WIDE), BF16),
        ((4, ROWS, 2 * HEAD), BF16),
        ((4, ROWS, 2 * HEAD), BF16),
        ((4, ROWS, HEAD), BF16),
        ((4, ROWS, HEAD), BF16),
        ((4, ROWS, WIDE), BF16),
        ((3, ROWS, 2 * HEAD), BF16),
        ((3, ROWS, 2 * HEAD), BF16),
        ((3, ROWS, HEAD), BF16),
        ((3, ROWS, HEAD), BF16),
        ((3, ROWS, WIDE), BF16),
        ((2, ROWS, 2 * HEAD), BF16),
        ((2, ROWS, HEAD), BF16),
        ((ROWS, WIDE), BF16),
    ]
    semaphores = 130
    anywhere = pl.BlockSpec(memory_space=pl.ANY)
    scalars = pl.BlockSpec(memory_space=pltpu.SMEM)
    vector = pl.BlockSpec(memory_space=pltpu.VMEM)
    return pl.pallas_call(
        layer_kernel,
        out_shape=(
            jax.ShapeDtypeStruct(full, BF16),
            jax.ShapeDtypeStruct(full, BF16),
            jax.ShapeDtypeStruct((ROWS, 2 * INNER), BF16),
            jax.ShapeDtypeStruct((ROWS, INNER), BF16),
            jax.ShapeDtypeStruct((ROWS, INNER), BF16),
        ),
        in_specs=[anywhere] * 4 + [scalars] * 2,
        out_specs=(vector,) * 5,
        scratch_shapes=[pltpu.VMEM(shape, dtype) for shape, dtype in scratch]
        + [
            pltpu.SemaphoreType.DMA((semaphores,)),
            pltpu.SemaphoreType.DMA((semaphores,)),
            pltpu.SemaphoreType.DMA((13,)),
        ],
        compiler_params=pltpu.CompilerParams(
            collective_id=0, has_side_effects=True, vmem_limit_bytes=VMEM_LIMIT
        ),
        name="whole_layer",
    )(tokens, upstream, w_qkv, w_out, key_blocks, key_count)


def finish_kernel(
    factor, layer_in, tokens_in, sum_a, sum_b, sum_out, layer_out, grad_tokens, grad_qkv, grad_out
):
    layer_out[...] = layer_in[...]
    grad_tokens[...] = tokens_in[...]
    for head in range(LOCAL_HEADS):
        cols = lanes(head)
        grad_qkv[:, cols] = sum_a[:, lanes(2 * head)].astype(F32) * factor
        grad_qkv[:, lanes(head + LOCAL_HEADS)] = sum_b[:, cols].astype(F32) * factor
        grad_qkv[:, lanes(head + 2 * LOCAL_HEADS)] = (
            sum_a[:, lanes(2 * head + 1)].astype(F32) * factor
        )
    grad_out[...] = sum_out[...].astype(F32) * factor


def finish(factor, *results):
    full = jax.ShapeDtypeStruct((TOK_DEV, D), BF16)
    vector = pl.BlockSpec(memory_space=pltpu.VMEM)
    return pl.pallas_call(
        functools.partial(finish_kernel, factor),
        out_shape=(
            full,
            full,
            jax.ShapeDtypeStruct((ROWS, 3 * INNER), F32),
            jax.ShapeDtypeStruct((ROWS, INNER), F32),
        ),
        in_specs=[vector] * 5,
        out_specs=(vector,) * 4,
        name="finish",
    )(*results)


def body(tokens, cotangent, w_qkv, w_out, key_blocks, key_count):
    factor = 1.0 / math.sqrt(lax.axis_size("dp") * lax.axis_size("seq") * TOK_DEV)
    results = whole_layer(
        tokens[0], cotangent[0], w_qkv, w_out, key_blocks.reshape(-1), key_count
    )
    layer_out, grad_tokens, grad_w_qkv, grad_w_out = finish(factor, *results)
    return (layer_out[None], grad_tokens[None], grad_w_qkv, grad_w_out)


def solution(mesh):
    return jax.shard_map(
        body,
        mesh=mesh,
        in_specs=(P("dp", "seq", None), P("dp", "seq", None), P(), P(), P(), P()),
        out_specs=(P("dp", "seq", None), P("dp", "seq", None), P("seq", None), P("seq", None)),
        check_vma=False,
    )
```

time: 425 us -> 109 us (0.26)
  waiting for transfers between devices: 274 us -> 0 us
  Pallas kernels: 0 us -> 107 us
  matrix products: 41.1 us -> 0 us
  starting transfers between devices: 33 us -> 0 us
  other arithmetic: 23.4 us -> 0 us
  local copies, waits for them, and re-layouts: 24.2 us -> 1.38 us
  loops' own time: 13.8 us -> 0 us
  between operations: 14.4 us -> 0.64 us
    reduce_scatter x1 -> x0, waiting for transfers between devices: 208 us -> none  [body(): lax.psum_scatter(jnp.concatenate([term_qkv, term_out], axis=1).astype(jnp...]
    pallas_call x0 -> x2, Pallas kernels: none -> 107 us  [the longest x1 105 us: whole_layer(): pl.pallas_call(layer_kernel, out_shape=(jax.ShapeDtypeStruct(full, BF16),...]
    psum x1 -> x0, waiting for transfers between devices: 56.4 us -> none  [body(): summed = lax.psum(shares, 'dp').astype(jnp.float32) * factor]
    dot_general x20 -> x0, matrix products: 41.1 us -> none  [the longest x1 8.9 us: body(): lax.dot_general(grad_qkv, w_qkv, contract_columns, preferred_element_type...]
    ppermute x4 -> x0, starting transfers between devices: 33 us -> none  [the longest x2 27.1 us: shifted(): lax.ppermute(value, axis, [(source, source + steps) for source in range(l...]
    another operation x3 -> x0, loops' own time: 13.8 us -> none  [the longest x1 4.72 us: attend_backward(): lax.fori_loop(0, total_pairs, back_pass, start_state)]
    concatenate x2 -> x0, other arithmetic: 9.3 us -> none  [the longest x1 9.19 us: body(): jnp.concatenate([term_qkv, term_out], axis=1).astype(jnp.bfloat16)]
    ppermute x4 -> x0, waiting for transfers between devices: 9.27 us -> none  [the longest x2 5.79 us: shifted(): lax.ppermute(value, axis, [(source, source + steps) for source in range(l...]
  transfers between devices with their start and end apart: 6 -> 0, of which waited for: 6 -> 0; matrix products, arithmetic and copies ran while one was open for 6% -> 0% of each run, Pallas kernels for 0% -> 0%
where the time goes in v2:
time: 109 us
  Pallas kernels  107 us (98%)
  local copies, waits for them, and re-layouts  1.38 us (1%)
    pallas_call x1, Pallas kernels, whole_layer(): pl.pallas_call(layer_kernel, out_shape=(jax.ShapeDtypeStruct(full, BF16),...  105 us
    pallas_call x1, Pallas kernels, finish(): pl.pallas_call(functools.partial(finish_kernel, factor), out_shape=(full,...  2.68 us

profile of v2, /device:TPU:1, one launch (start us, length us, event | category | flops | bytes accessed | tf_op | source)
XLA Modules:
  0.0 109.3 jit_solution(11494119630628267769)
XLA Ops:
  0.6 0.8 copy.11
  1.4 0.6 reshape.11.key_blocks
  2.0 104.6 %whole_layer.1 = (bf16[128,2048]{1,0:T(8,128)(2,1)}, bf16[128,2048]{1,0:T(8,128)(2,1)}, bf16[64,2048]{1,0:T(8,128)(2,1)}, bf16[64,1024]{1,0:T(8,128)(2,1)}, bf16[64,1024]{1,0:T(8,128)(2,1)}) custom-call(bf16[128,2048]{1,0:T(8,128)(2,1)} %bitcast.4, bf16[128,2048]{1,0:T(8,128)(2,1)} %bitcast.5, bf16[2048,3072]{1,0:T(8,128)(2,1)} %w_qkv_hbm.1, ...), custom_call_target="tpu_custom_call" | custom-call | tf_op jit(solution)/shard_map/whole_layer/pallas_call | solution.py:753
  106.6 2.7 %finish.1 = (bf16[128,2048]{1,0:T(8,128)(2,1)}, bf16[128,2048]{1,0:T(8,128)(2,1)}, f32[64,3072]{1,0:T(8,128)}, f32[64,1024]{1,0:T(8,128)}) custom-call(bf16[128,2048]{1,0:T(8,128)(2,1)} %get-tuple-element.13.layer_in, bf16[128,2048]{1,0:T(8,128)(2,1)} %get-tuple-element.14.tokens_in, bf16[64,2048]{1,0:T(8,128)(2,1)} %get-tuple-element.15.sum_a, ...), custom_call_target="tpu_custom_call" | custom-call | tf_op jit(solution)/shard_map/finish/pallas_call | solution.py:795

commit v3 on v2

--- a/solution.py
+++ b/solution.py
@@ -19,6 +19,7 @@
 WINDOW = 3 * TOK_DEV
 ALL_TOK = GROUP * TOK_DEV
 ROWS = D // N_SEQ
+HALF_ROWS = ROWS // 2
 WIDE = 256
 VMEM_LIMIT = 63 * 1024 * 1024
 
@@ -29,7 +30,7 @@
 CONTRACT_COLUMNS = (((1,), (1,)), ((), ()))
 CONTRACT_ROWS = (((0,), (0,)), ((), ()))
 STEPS = range(1, RING)
-Z_GROUP = [(o, other) for o in range(RING) for other in range(2) if o + other]
+GROUP_STEPS = [(o, other) for o in range(RING) for other in range(2) if o + other]
 
 
 def place():
@@ -86,27 +87,37 @@
         )
 
 
-def ring_gather(copies, view, up, down, partner):
-    from_down = copies.start(view(0, None), view(2, None), up)
-    from_up = copies.start(view(0, None), view(6, None), down)
-    rest = [copies.start(view(0, None), view(1, None), partner)]
-    yield
-    from_down.wait_recv()
-    far_low = copies.start(view(2, 0), view(4, 0), up)
-    from_up.wait_recv()
-    far_high = copies.start(view(6, 1), view(4, 1), down)
-    rest.append(copies.start(view(2, None), view(3, None), partner))
-    rest.append(copies.start(view(6, None), view(7, None), partner))
-    yield
-    far_low.wait_recv()
-    rest.append(copies.start(view(4, 0), view(5, 0), partner))
-    far_high.wait_recv()
-    rest.append(copies.start(view(4, 1), view(5, 1), partner))
-    yield
-    wait_all(rest)
-    for copy in (from_down, from_up, far_low, far_high):
-        copy.wait_send()
-    yield
+class RingGather:
+    def __init__(self, copies, slot, fast, slow, partner):
+        self.copies, self.slot = copies, slot
+        self.fast, self.slow, self.partner = fast, slow, partner
+        self.waits, self.back = [], []
+
+    def start(self, src, dst, device, part=None):
+        return self.copies.start(self.slot(src, part), self.slot(dst, part), device)
+
+    def begin(self):
+        self.near = self.start(0, 2, self.fast)
+        self.waits.append(self.start(0, 1, self.partner))
+
+    def pass_on(self):
+        self.near.wait()
+        self.far = self.start(2, 4, self.fast)
+        self.waits.append(self.start(2, 3, self.partner))
+
+    def begin_slow(self, part):
+        self.back.append(self.start(0, 6, self.slow, part))
+
+    def share_far(self):
+        self.far.wait()
+        self.waits.append(self.start(4, 5, self.partner))
+
+    def share_back(self):
+        wait_all(self.back)
+        self.waits.append(self.start(6, 7, self.partner))
+
+    def end(self):
+        wait_all(self.waits)
 
 
 def added(first, *others):
@@ -162,18 +173,18 @@
     part_b,
     part_out,
     x_first_a,
-    y_first_a,
+    z_first_a,
     x_first_b,
-    y_first_b,
+    z_first_b,
     y_first_out,
     x_summed_a,
-    y_summed_a,
+    z_summed_a,
     x_summed_b,
-    y_summed_b,
+    z_summed_b,
     y_summed_out,
-    then_y_a,
+    then_z_a,
     then_x_a,
-    then_y_b,
+    then_z_b,
     then_x_b,
     then_x_out,
     whole_a,
@@ -186,26 +197,29 @@
     x, y, z, c = place()
     dp, seq = lax.axis_index("dp"), lax.axis_index("seq")
     z_hi, z_lo = z // 2, z % 2
-    mine = z * 2 + c
+    mine = y * 2 + c
+    sign = jnp.where(x < 2, -1, 1)
     following = {"dp": dp, "seq": (seq + 1) % N_SEQ}
     preceding = {"dp": dp, "seq": (seq + N_SEQ - 1) % N_SEQ}
     has_after, has_before = seq < N_SEQ - 1, seq > 0
     scale = HEAD ** (-0.5)
     copies = Copies(send, recv)
 
-    loads = {}
-    for i, (name, src, dst) in enumerate(
-        [
-            ("tokens", tokens_hbm, tokens),
-            ("keys", w_qkv_hbm.at[:, pl.ds(INNER, INNER)], w_keys),
-            ("values", w_qkv_hbm.at[:, pl.ds(2 * INNER, INNER)], w_values),
-            ("upstream", upstream_hbm, upstream),
-            ("query", w_qkv_hbm.at[:, pl.ds(0, INNER)], w_query),
-            ("out", w_out_hbm, w_out),
-        ]
-    ):
-        loads[name] = pltpu.make_async_copy(src, dst, local.at[i])
-        loads[name].start()
+    loads = {
+        name: pltpu.make_async_copy(src, dst, local.at[i])
+        for i, (name, src, dst) in enumerate(
+            [
+                ("tokens", tokens_hbm, tokens),
+                ("keys", w_qkv_hbm.at[:, pl.ds(INNER, INNER)], w_keys),
+                ("values", w_qkv_hbm.at[:, pl.ds(2 * INNER, INNER)], w_values),
+                ("upstream", upstream_hbm, upstream),
+                ("query", w_qkv_hbm.at[:, pl.ds(0, INNER)], w_query),
+                ("out", w_out_hbm, w_out),
+            ]
+        )
+    }
+    loads["tokens"].start()
+    loads["keys"].start()
 
     peers = [
         at(x, (y + o) % 4, z_hi * 2 + (z_lo + lo) % 2, (c + other) % 2)
@@ -232,7 +246,7 @@
         from_after[...] = zero_block
 
     count = key_count[seq]
-    listed = [key_blocks[seq * 3 + j] for j in range(3)]
+    listed = [key_blocks[seq, j] for j in range(3)]
     biases = []
     for shift in (-1, 0, 1):
         used = jnp.int32(0)
@@ -244,6 +258,7 @@
     bias = jnp.concatenate(biases, axis=1)
 
     loads["tokens"].wait()
+    loads["values"].start()
     wide_tokens = tokens[...].astype(F32)
     inv_rms[...] = lax.rsqrt(jnp.mean(wide_tokens * wide_tokens, axis=1, keepdims=True) + epsilon)
     normed[...] = (wide_tokens * inv_rms[...]).astype(BF16)
@@ -288,14 +303,6 @@
         def _():
             back.wait_send()
             forth.wait_recv()
-
-    loads["keys"].wait()
-    project(normed, w_keys, kv, 0)
-    pl.semaphore_wait(pltpu.get_barrier_semaphore(), len(peers))
-    send_halo(0)
-    loads["values"].wait()
-    project(normed, w_values, kv, INNER // WIDE)
-    send_halo(1)
 
     def turn(rows, out):
         def chunk(i, carry):
@@ -306,41 +313,63 @@
 
         lax.fori_loop(0, D // WIDE, chunk, 0)
 
+    def exchange_y(src_view, dst_view):
+        sent = []
+        for o, other in GROUP_STEPS:
+            to, core = (y + sign * o + 4) % 4, (c + other) % 2
+            sent.append(
+                copies.start(src_view(to, core), dst_view(2 * o + other), at(x, to, z, core))
+            )
+        return sent
+
+    def exchange_z(src_view, dst_view):
+        sent = []
+        for o, other in GROUP_STEPS:
+            to, core = (z + o) % 4, (c + other) % 2
+            sent.append(
+                copies.start(src_view(to, core), dst_view(2 * o + other), at(x, y, to, core))
+            )
+        return sent
+
     partner = at(x, y, z, 1 - c)
-    z_up, z_down = at(x, y, (z + 1) % 4, c), at(x, y, (z + 3) % 4, c)
-
-    def in_z(o, other):
-        return (z + o) % 4, (c + other) % 2
-
-    def normed_view(slot, part):
+    fast, slow = at(x, (y + sign + 4) % 4, z, c), at(x, (y - sign + 4) % 4, z, c)
+
+    def normed_slot(slot, part):
         rows = pl.ds(0, D) if part is None else pl.ds(part * (D // 2), D // 2)
         return all_normed.at[rows, lanes(slot)]
 
-    def attended_view(slot, part):
+    def attended_slot(slot, part):
         cols = pl.ds(0, INNER) if part is None else pl.ds(part * (INNER // 2), INNER // 2)
         return all_attended.at[lanes(slot), cols]
 
-    def exchange(src_view, dst_view):
-        sent = []
-        for o, other in Z_GROUP:
-            to, core = in_z(o, other)
-            sent.append(
-                copies.start(src_view(to * 2 + core), dst_view(2 * o + other), at(x, y, to, core))
-            )
-        return sent
+    normed_ring = RingGather(copies, normed_slot, fast, slow, partner)
+    attended_ring = RingGather(
+        copies,
+        attended_slot,
+        at(x, y, (z + 1) % 4, c),
+        at(x, y, (z + 3) % 4, c),
+        partner,
+    )
 
     turn(normed, all_normed)
-    normed_ring = ring_gather(copies, normed_view, z_up, z_down, partner)
-    next(normed_ring)
+    pl.semaphore_wait(pltpu.get_barrier_semaphore(), len(peers))
+    normed_ring.begin()
+    normed_ring.begin_slow(0)
+    loads["keys"].wait()
+    loads["upstream"].start()
+    loads["query"].start()
+    project(normed, w_keys, kv, 0)
+    send_halo(0)
+    loads["values"].wait()
+    loads["out"].start()
+    project(normed, w_values, kv, INNER // WIDE)
+    send_halo(1)
     loads["upstream"].wait()
     turn(upstream, upstream_t)
 
-    def turned(index):
-        return upstream_t.at[pl.ds(pl.multiple_of(index * WIDE, WIDE), WIDE), :]
-
-    keep = [pltpu.make_async_copy(turned(mine), cot_rows.at[:, lanes(0)], local.at[6])]
-    keep[0].start()
-    sent_cot = exchange(turned, lambda slot: cot_rows.at[:, lanes(slot)])
+    def turned(to, core):
+        return upstream_t.at[lanes(to * 2 + core, WIDE), :]
+
     loads["query"].wait()
     project(normed, w_query, query, 0)
     loads["out"].wait()
@@ -448,7 +477,9 @@
 
     take_halo(0)
     lax.fori_loop(0, pair_count, pairs(weigh), 0)
+    normed_ring.pass_on()
     take_halo(1)
+    normed_ring.begin_slow(1)
 
     def attend_pair(i, carry):
         pairs(attend)(i, carry)
@@ -457,9 +488,8 @@
 
     lax.fori_loop(0, pair_count, attend_pair, 0)
     all_attended[pl.ds(0, TOK_DEV), :] = attended[...]
-    next(normed_ring)
-    attended_ring = ring_gather(copies, attended_view, z_up, z_down, partner)
-    next(attended_ring)
+    attended_ring.begin()
+    attended_ring.begin_slow(None)
 
     def back_pair(i, carry):
         pairs(attend_back)(i, carry)
@@ -473,8 +503,9 @@
             src.at[:, lanes(mine)], dst.at[pl.ds(0, TOK_DEV), cols], local.at[i]
         )
         stay.start()
-        return [stay] + exchange(
-            lambda index: src.at[:, lanes(index)], lambda slot: dst.at[lanes(slot), cols]
+        return [stay] + exchange_y(
+            lambda to, core: src.at[:, lanes(to * 2 + core)],
+            lambda slot: dst.at[lanes(slot), cols],
         )
 
     sent_query = swap_columns(grad_query, grads_a, pl.ds(0, HEAD), 7)
@@ -489,12 +520,10 @@
         return carry
 
     lax.fori_loop(0, D // WIDE, out_chunk, 0)
-    next(normed_ring)
-    next(attended_ring)
-
     take_back(pair_count)
     settle(grad_values, INNER)
     sent_values = swap_columns(grad_values, grads_a, pl.ds(HEAD, HEAD), 8)
+    attended_ring.pass_on()
 
     def grad_chunk_a(i, carry):
         rows = pl.ds(pl.multiple_of(i * WIDE, WIDE), WIDE)
@@ -506,72 +535,121 @@
         return carry
 
     lax.fori_loop(0, D // WIDE, grad_chunk_a, 0)
+    normed_ring.share_far()
     take_back(0)
     settle(grad_keys, 0)
     sent_keys = swap_columns(grad_keys, grads_b, pl.ds(0, HEAD), 9)
-    next(normed_ring)
-    next(attended_ring)
-
-    def multiply(grads, part, width, first):
+    keep = [pltpu.make_async_copy(turned(z, c), cot_rows.at[:, lanes(0)], local.at[6])]
+    keep[0].start()
+    sent_cot = exchange_z(turned, lambda slot: cot_rows.at[:, lanes(slot)])
+    normed_ring.share_back()
+    attended_ring.share_back()
+    attended_ring.share_far()
+    normed_ring.end()
+
+    def multiply(grads, part, width):
         def chunk(i, carry):
             rows = pl.ds(pl.multiple_of(i * WIDE, WIDE), WIDE)
             product = jnp.dot(all_normed[rows, :], grads[...], preferred_element_type=F32)
-            part[i] = product.astype(BF16).reshape(4, ROWS, width)
+            part[i // 4, i % 4] = product.astype(BF16).reshape(4, ROWS, width)
             return carry
 
-        lax.fori_loop(first, first + 4, chunk, 0)
-
-    def scatter(grads, part, width, x_first, y_first):
-        multiply(grads, part, width, 0)
-        x_sent = [
-            copies.start(
-                part.at[pl.ds(0, 4), (x + o) % 4], x_first.at[o - 1], at((x + o) % 4, y, z, c)
+        lax.fori_loop(0, D // WIDE, chunk, 0)
+
+    def half(lo):
+        return pl.ds(pl.multiple_of(lo * HALF_ROWS, HALF_ROWS), HALF_ROWS)
+
+    first_y, last_y = pl.ds(0, 2), pl.ds(2, 2)
+
+    def scatter(grads, part, width, x_first, z_first):
+        multiply(grads, part, width)
+        x_sent, z_sent = [], []
+        for o in STEPS:
+            to = (x + o) % 4
+            x_sent.append(
+                copies.start(part.at[:, first_y, to], x_first.at[o - 1], at(to, y, z, c))
             )
+            to = (z + o) % 4
+            z_sent.append(
+                copies.start(
+                    part.at[to // 2, last_y, :, half(to % 2)], z_first.at[o - 1], at(x, y, to, c)
+                )
+            )
+        return x_sent, z_sent
+
+    def scatter_on(sent, part, x_first, z_first, x_summed, z_summed, then_z, then_x):
+        x_sent, z_sent = sent
+        wait_all(x_sent)
+        x_summed[...] = added(part[:, first_y, x], x_first[0], x_first[1], x_first[2])
+        z_then = []
+        for o in STEPS:
+            to = (z + o) % 4
+            z_then.append(
+                copies.start(
+                    x_summed.at[to // 2, :, half(to % 2)], then_z.at[o - 1], at(x, y, to, c)
+                )
+            )
+        wait_all(z_sent)
+        z_summed[...] = added(
+            part[z_hi, last_y, :, half(z_lo)], z_first[0], z_first[1], z_first[2]
+        )
+        x_then = [
+            copies.start(z_summed.at[:, (x + o) % 4], then_x.at[o - 1], at((x + o) % 4, y, z, c))
             for o in STEPS
         ]
-        multiply(grads, part, width, 4)
-        y_sent = [
-            copies.start(part.at[4 + (y + o) % 4], y_first.at[o - 1], at(x, (y + o) % 4, z, c))
-            for o in STEPS
-        ]
-        return x_sent, y_sent
-
-    def scatter_on(sent, part, x_first, y_first, x_summed, y_summed, then_y, then_x):
-        x_sent, y_sent = sent
-        wait_all(x_sent)
-        x_summed[...] = added(part[0:4, x], x_first[0], x_first[1], x_first[2])
-        y_then = [
-            copies.start(x_summed.at[(y + o) % 4], then_y.at[o - 1], at(x, (y + o) % 4, z, c))
-            for o in STEPS
-        ]
-        wait_all(y_sent)
-        y_summed[...] = added(part[4 + y], y_first[0], y_first[1], y_first[2])
-        x_then = [
-            copies.start(y_summed.at[(x + o) % 4], then_x.at[o - 1], at((x + o) % 4, y, z, c))
-            for o in STEPS
-        ]
-        return y_then, x_then
-
-    def gather_sums(sent, x_summed, y_summed, then_y, then_x, whole, out, width, i):
-        y_then, x_then = sent
-        wait_all(y_then)
-        whole[0] = added(x_summed[y], then_y[0], then_y[1], then_y[2])
+        return z_then, x_then
+
+    finals = [
+        (o, lo, other)
+        for o in range(RING)
+        for lo in range(2)
+        for other in range(2)
+        if o + lo + other
+    ]
+
+    def gather_sums(sent, x_summed, z_summed, then_z, then_x, whole, out, width, i):
+        z_then, x_then = sent
+        wait_all(z_then)
+        whole[first_y] = added(x_summed[z_hi, :, half(z_lo)], then_z[0], then_z[1], then_z[2])
         wait_all(x_then)
-        whole[1] = added(y_summed[x], then_x[0], then_x[1], then_x[2])
-        own_place = out.at[:, lanes(mine, width)]
-        stay = pltpu.make_async_copy(whole.at[z_hi], own_place, local.at[i])
+        whole[last_y] = added(z_summed[:, x], then_x[0], then_x[1], then_x[2])
+        own_place = out.at[half(z_lo), lanes(mine, width)]
+        stay = pltpu.make_async_copy(whole.at[y], own_place, local.at[i])
         stay.start()
         last = [stay]
-        for o, other in Z_GROUP:
-            to, core = in_z(o, other)
-            last.append(copies.start(whole.at[to // 2], own_place, at(x, y, to, core)))
+        for o, lo, other in finals:
+            to = (y + o) % 4
+            device = at(x, to, z_hi * 2 + (z_lo + lo) % 2, (c + other) % 2)
+            last.append(copies.start(whole.at[to], own_place, device))
         return last
 
     wait_all(sent_query + sent_values)
-    sent_a = scatter(grads_a, part_a, 2 * HEAD, x_first_a, y_first_a)
+    sent_a = scatter(grads_a, part_a, 2 * HEAD, x_first_a, z_first_a)
+
+    wait_all(sent_keys)
+    sent_b = scatter(grads_b, part_b, HEAD, x_first_b, z_first_b)
+
+    def grad_chunk_b(i, total):
+        rows, cols = pl.ds(pl.multiple_of(i * WIDE, WIDE), WIDE), lanes(i, WIDE)
+        product = grad_normed[:, cols] + lax.dot_general(
+            grad_keys[...], w_keys[rows, :], CONTRACT_COLUMNS, preferred_element_type=F32
+        )
+        grad_normed[:, cols] = product
+        along = product * (tokens[:, cols].astype(F32) * inv_rms[...])
+        return total + jnp.sum(along, axis=1, keepdims=True)
+
+    total = lax.fori_loop(0, D // WIDE, grad_chunk_b, jnp.zeros((TOK_DEV, 1), F32))
+    mean = total * (1.0 / D)
+
+    def tokens_chunk(i, carry):
+        cols = lanes(i, WIDE)
+        normed_wide = tokens[:, cols].astype(F32) * inv_rms[...]
+        branch = inv_rms[...] * (grad_normed[:, cols] - normed_wide * mean)
+        grad_tokens[:, cols] = (upstream[:, cols].astype(F32) + branch).astype(BF16)
+        return carry
 
     wait_all(keep + sent_cot)
-    next(attended_ring)
+    attended_ring.end()
 
     def out_part(i, carry):
         cols = lanes(i, WIDE)
@@ -588,31 +666,8 @@
         )
         for o in STEPS
     ]
-
-    wait_all(sent_keys)
-    sent_b = scatter(grads_b, part_b, HEAD, x_first_b, y_first_b)
-
-    def grad_chunk_b(i, total):
-        rows, cols = pl.ds(pl.multiple_of(i * WIDE, WIDE), WIDE), lanes(i, WIDE)
-        product = grad_normed[:, cols] + lax.dot_general(
-            grad_keys[...], w_keys[rows, :], CONTRACT_COLUMNS, preferred_element_type=F32
-        )
-        grad_normed[:, cols] = product
-        along = product * (tokens[:, cols].astype(F32) * inv_rms[...])
-        return total + jnp.sum(along, axis=1, keepdims=True)
-
-    total = lax.fori_loop(0, D // WIDE, grad_chunk_b, jnp.zeros((TOK_DEV, 1), F32))
-    mean = total * (1.0 / D)
-
-    def tokens_chunk(i, carry):
-        cols = lanes(i, WIDE)
-        normed_wide = tokens[:, cols].astype(F32) * inv_rms[...]
-        branch = inv_rms[...] * (grad_normed[:, cols] - normed_wide * mean)
-        grad_tokens[:, cols] = (upstream[:, cols].astype(F32) + branch).astype(BF16)
-        return carry
-
     then_a = scatter_on(
-        sent_a, part_a, x_first_a, y_first_a, x_summed_a, y_summed_a, then_y_a, then_x_a
+        sent_a, part_a, x_first_a, z_first_a, x_summed_a, z_summed_a, then_z_a, then_x_a
     )
     wait_all(y_sent_out)
     y_summed_out[...] = added(
@@ -626,10 +681,10 @@
     ]
     lax.fori_loop(0, D // WIDE, tokens_chunk, 0)
     then_b = scatter_on(
-        sent_b, part_b, x_first_b, y_first_b, x_summed_b, y_summed_b, then_y_b, then_x_b
+        sent_b, part_b, x_first_b, z_first_b, x_summed_b, z_summed_b, then_z_b, then_x_b
     )
     last = gather_sums(
-        then_a, x_summed_a, y_summed_a, then_y_a, then_x_a, whole_a, sum_a, 2 * HEAD, 10
+        then_a, x_summed_a, z_summed_a, then_z_a, then_x_a, whole_a, sum_a, 2 * HEAD, 10
     )
 
     wait_all(x_then_out)
@@ -663,7 +718,7 @@
         stay.wait()
 
     last += gather_sums(
-        then_b, x_summed_b, y_summed_b, then_y_b, then_x_b, whole_b, sum_b, HEAD, 11
+        then_b, x_summed_b, z_summed_b, then_z_b, then_x_b, whole_b, sum_b, HEAD, 11
     )
     for copy in outgoing[1:]:
         copy.wait_send()
@@ -724,29 +779,29 @@
         (full, F32),
         ((ALL_TOK, 2 * HEAD), BF16),
         ((ALL_TOK, HEAD), BF16),
-        ((8, 4, ROWS, 2 * HEAD), BF16),
-        ((8, 4, ROWS, HEAD), BF16),
+        ((2, 4, 4, ROWS, 2 * HEAD), BF16),
+        ((2, 4, 4, ROWS, HEAD), BF16),
         ((4, ROWS, INNER), BF16),
-        ((3, 4, ROWS, 2 * HEAD), BF16),
-        ((3, 4, ROWS, 2 * HEAD), BF16),
-        ((3, 4, ROWS, HEAD), BF16),
-        ((3, 4, ROWS, HEAD), BF16),
+        ((3, 2, 2, ROWS, 2 * HEAD), BF16),
+        ((3, 2, 4, HALF_ROWS, 2 * HEAD), BF16),
+        ((3, 2, 2, ROWS, HEAD), BF16),
+        ((3, 2, 4, HALF_ROWS, HEAD), BF16),
         ((3, 4, ROWS, WIDE), BF16),
-        ((4, ROWS, 2 * HEAD), BF16),
-        ((4, ROWS, 2 * HEAD), BF16),
-        ((4, ROWS, HEAD), BF16),
-        ((4, ROWS, HEAD), BF16),
+        ((2, 2, ROWS, 2 * HEAD), BF16),
+        ((2, 4, HALF_ROWS, 2 * HEAD), BF16),
+        ((2, 2, ROWS, HEAD), BF16),
+        ((2, 4, HALF_ROWS, HEAD), BF16),
         ((4, ROWS, WIDE), BF16),
-        ((3, ROWS, 2 * HEAD), BF16),
-        ((3, ROWS, 2 * HEAD), BF16),
-        ((3, ROWS, HEAD), BF16),
-        ((3, ROWS, HEAD), BF16),
+        ((3, 2, HALF_ROWS, 2 * HEAD), BF16),
+        ((3, 2, HALF_ROWS, 2 * HEAD), BF16),
+        ((3, 2, HALF_ROWS, HEAD), BF16),
+        ((3, 2, HALF_ROWS, HEAD), BF16),
         ((3, ROWS, WIDE), BF16),
-        ((2, ROWS, 2 * HEAD), BF16),
-        ((2, ROWS, HEAD), BF16),
+        ((4, HALF_ROWS, 2 * HEAD), BF16),
+        ((4, HALF_ROWS, HEAD), BF16),
         ((ROWS, WIDE), BF16),
     ]
-    semaphores = 130
+    semaphores = 140
     anywhere = pl.BlockSpec(memory_space=pl.ANY)
     scalars = pl.BlockSpec(memory_space=pltpu.SMEM)
     vector = pl.BlockSpec(memory_space=pltpu.VMEM)
@@ -809,7 +864,7 @@
 def body(tokens, cotangent, w_qkv, w_out, key_blocks, key_count):
     factor = 1.0 / math.sqrt(lax.axis_size("dp") * lax.axis_size("seq") * TOK_DEV)
     results = whole_layer(
-        tokens[0], cotangent[0], w_qkv, w_out, key_blocks.reshape(-1), key_count
+        tokens[0], cotangent[0], w_qkv, w_out, key_blocks, key_count
     )
     layer_out, grad_tokens, grad_w_qkv, grad_w_out = finish(factor, *results)
     return (layer_out[None], grad_tokens[None], grad_w_qkv, grad_w_out)

time: 109 us -> 87.5 us (0.80)
  Pallas kernels: 107 us -> 85.3 us
    pallas_call x1, Pallas kernels: 105 us -> 82.6 us  [whole_layer(): pl.pallas_call(layer_kernel, out_shape=(jax.ShapeDtypeStruct(full, BF16),...]
where the time goes in v3:
time: 87.5 us; the launch traced here: 87.3 us
  Pallas kernels  85.3 us (97%)
  local copies, waits for them, and re-layouts  1.37 us (2%)
    pallas_call x1, Pallas kernels, whole_layer(): pl.pallas_call(layer_kernel, out_shape=(jax.ShapeDtypeStruct(full, BF16),...  82.6 us
    pallas_call x1, Pallas kernels, finish(): pl.pallas_call(functools.partial(finish_kernel, factor), out_shape=(full,...  2.68 us

profile of v3, /device:TPU:1, one launch (start us, length us, event | category | flops | bytes accessed | tf_op | source)
XLA Modules:
  0.0 87.3 jit_solution(13597444842307851016)
XLA Ops:
  0.6 1.4 %copy.10.key_blocks = s32[32,3]{1,0:T(8,128)} copy(s32[32,3]{0,1:T(4,128)} %param.10) | data formatting | bytes 768 | tf_op args[4]
  2.0 82.6 %whole_layer.1 = (bf16[128,2048]{1,0:T(8,128)(2,1)}, bf16[128,2048]{1,0:T(8,128)(2,1)}, bf16[64,2048]{1,0:T(8,128)(2,1)}, bf16[64,1024]{1,0:T(8,128)(2,1)}, bf16[64,1024]{1,0:T(8,128)(2,1)}) custom-call(bf16[128,2048]{1,0:T(8,128)(2,1)} %bitcast.4, bf16[128,2048]{1,0:T(8,128)(2,1)} %bitcast.5, bf16[2048,3072]{1,0:T(8,128)(2,1)} %w_qkv_hbm.1, ...), custom_call_target="tpu_custom_call" | custom-call | tf_op jit(solution)/shard_map/whole_layer/pallas_call | solution.py:808
  84.6 2.7 %finish.1 = (bf16[128,2048]{1,0:T(8,128)(2,1)}, bf16[128,2048]{1,0:T(8,128)(2,1)}, f32[64,3072]{1,0:T(8,128)}, f32[64,1024]{1,0:T(8,128)}) custom-call(bf16[128,2048]{1,0:T(8,128)(2,1)} %get-tuple-element.13.layer_in, bf16[128,2048]{1,0:T(8,128)(2,1)} %get-tuple-element.14.tokens_in, bf16[64,2048]{1,0:T(8,128)(2,1)} %get-tuple-element.15.sum_a, ...), custom_call_target="tpu_custom_call" | custom-call | tf_op jit(solution)/shard_map/finish/pallas_call | solution.py:850

commit v4 on v3

--- a/solution.py
+++ b/solution.py
@@ -246,7 +246,7 @@
         from_after[...] = zero_block
 
     count = key_count[seq]
-    listed = [key_blocks[seq, j] for j in range(3)]
+    listed = [key_blocks[j, seq] for j in range(3)]
     biases = []
     for shift in (-1, 0, 1):
         used = jnp.int32(0)
@@ -846,17 +846,25 @@
 
 def finish(factor, *results):
     full = jax.ShapeDtypeStruct((TOK_DEV, D), BF16)
-    vector = pl.BlockSpec(memory_space=pltpu.VMEM)
+    outs = (
+        full,
+        full,
+        jax.ShapeDtypeStruct((ROWS, 3 * INNER), F32),
+        jax.ShapeDtypeStruct((ROWS, INNER), F32),
+    )
+    steps = 2
+
+    def blocks(arrays):
+        return tuple(
+            pl.BlockSpec((a.shape[0] // steps, a.shape[1]), lambda i: (i, 0)) for a in arrays
+        )
+
     return pl.pallas_call(
         functools.partial(finish_kernel, factor),
-        out_shape=(
-            full,
-            full,
-            jax.ShapeDtypeStruct((ROWS, 3 * INNER), F32),
-            jax.ShapeDtypeStruct((ROWS, INNER), F32),
-        ),
-        in_specs=[vector] * 5,
-        out_specs=(vector,) * 4,
+        grid=(steps,),
+        out_shape=outs,
+        in_specs=blocks(results),
+        out_specs=blocks(outs),
         name="finish",
     )(*results)
 
@@ -864,7 +872,7 @@
 def body(tokens, cotangent, w_qkv, w_out, key_blocks, key_count):
     factor = 1.0 / math.sqrt(lax.axis_size("dp") * lax.axis_size("seq") * TOK_DEV)
     results = whole_layer(
-        tokens[0], cotangent[0], w_qkv, w_out, key_blocks, key_count
+        tokens[0], cotangent[0], w_qkv, w_out, key_blocks.T, key_count
     )
     layer_out, grad_tokens, grad_w_qkv, grad_w_out = finish(factor, *results)
     return (layer_out[None], grad_tokens[None], grad_w_qkv, grad_w_out)

time: 87.5 us -> 85.7 us (0.979)
  local copies, waits for them, and re-layouts: 1.37 us -> 0 us
    unnamed x1 -> x0, local copies, waits for them, and re-layouts: 1.37 us -> none
where the time goes in v4:
time: 85.7 us; the launch traced here: 85.5 us
  Pallas kernels  84.9 us (99%)
    pallas_call x1, Pallas kernels, whole_layer(): pl.pallas_call(layer_kernel, out_shape=(jax.ShapeDtypeStruct(full, BF16),...  82.4 us
    pallas_call x1, Pallas kernels, finish(): pl.pallas_call(functools.partial(finish_kernel, factor), grid=(steps,), o...  2.47 us

profile of v4, /device:TPU:1, one launch (start us, length us, event | category | flops | bytes accessed | tf_op | source)
XLA Modules:
  0.0 85.5 jit_solution(7695638269615727671)
XLA Ops:
  0.6 82.4 %whole_layer.1 = (bf16[128,2048]{1,0:T(8,128)(2,1)}, bf16[128,2048]{1,0:T(8,128)(2,1)}, bf16[64,2048]{1,0:T(8,128)(2,1)}, bf16[64,1024]{1,0:T(8,128)(2,1)}, bf16[64,1024]{1,0:T(8,128)(2,1)}) custom-call(bf16[128,2048]{1,0:T(8,128)(2,1)} %bitcast.5, bf16[128,2048]{1,0:T(8,128)(2,1)} %bitcast.6, bf16[2048,3072]{1,0:T(8,128)(2,1)} %w_qkv_hbm.1, ...), custom_call_target="tpu_custom_call" | custom-call | tf_op jit(solution)/shard_map/whole_layer/pallas_call | solution.py:808
  83.0 2.5 %finish.1 = (bf16[128,2048]{1,0:T(8,128)(2,1)}, bf16[128,2048]{1,0:T(8,128)(2,1)}, f32[64,3072]{1,0:T(8,128)}, f32[64,1024]{1,0:T(8,128)}) custom-call(bf16[128,2048]{1,0:T(8,128)(2,1)} %get-tuple-element.13.layer_in, bf16[128,2048]{1,0:T(8,128)(2,1)} %get-tuple-element.14.tokens_in, bf16[64,2048]{1,0:T(8,128)(2,1)} %get-tuple-element.15.sum_a, ...), custom_call_target="tpu_custom_call" | custom-call | tf_op jit(solution)/shard_map/finish/pallas_call | solution.py:862

commit v5 on v4

--- a/solution.py
+++ b/solution.py
@@ -258,7 +258,6 @@
     bias = jnp.concatenate(biases, axis=1)
 
     loads["tokens"].wait()
-    loads["values"].start()
     wide_tokens = tokens[...].astype(F32)
     inv_rms[...] = lax.rsqrt(jnp.mean(wide_tokens * wide_tokens, axis=1, keepdims=True) + epsilon)
     normed[...] = (wide_tokens * inv_rms[...]).astype(BF16)
@@ -356,11 +355,12 @@
     normed_ring.begin()
     normed_ring.begin_slow(0)
     loads["keys"].wait()
+    loads["values"].start()
     loads["upstream"].start()
-    loads["query"].start()
     project(normed, w_keys, kv, 0)
     send_halo(0)
     loads["values"].wait()
+    loads["query"].start()
     loads["out"].start()
     project(normed, w_values, kv, INNER // WIDE)
     send_halo(1)

time: 85.7 us -> 85.7 us (level)
  no operation moved by 1% of the time
where the time goes in v5:
time: 85.7 us; the launch traced here: 85.5 us
  Pallas kernels  84.9 us (99%)
    pallas_call x1, Pallas kernels, whole_layer(): pl.pallas_call(layer_kernel, out_shape=(jax.ShapeDtypeStruct(full, BF16),...  82.4 us
    pallas_call x1, Pallas kernels, finish(): pl.pallas_call(functools.partial(finish_kernel, factor), grid=(steps,), o...  2.47 us

profile of v5, /device:TPU:1, one launch (start us, length us, event | category | flops | bytes accessed | tf_op | source)
XLA Modules:
  0.0 85.5 jit_solution(13944555944741927669)
XLA Ops:
  0.6 82.4 %whole_layer.1 = (bf16[128,2048]{1,0:T(8,128)(2,1)}, bf16[128,2048]{1,0:T(8,128)(2,1)}, bf16[64,2048]{1,0:T(8,128)(2,1)}, bf16[64,1024]{1,0:T(8,128)(2,1)}, bf16[64,1024]{1,0:T(8,128)(2,1)}) custom-call(bf16[128,2048]{1,0:T(8,128)(2,1)} %bitcast.5, bf16[128,2048]{1,0:T(8,128)(2,1)} %bitcast.6, bf16[2048,3072]{1,0:T(8,128)(2,1)} %w_qkv_hbm.1, ...), custom_call_target="tpu_custom_call" | custom-call | tf_op jit(solution)/shard_map/whole_layer/pallas_call | solution.py:808
  83.1 2.5 %finish.1 = (bf16[128,2048]{1,0:T(8,128)(2,1)}, bf16[128,2048]{1,0:T(8,128)(2,1)}, f32[64,3072]{1,0:T(8,128)}, f32[64,1024]{1,0:T(8,128)}) custom-call(bf16[128,2048]{1,0:T(8,128)(2,1)} %get-tuple-element.13.layer_in, bf16[128,2048]{1,0:T(8,128)(2,1)} %get-tuple-element.14.tokens_in, bf16[64,2048]{1,0:T(8,128)(2,1)} %get-tuple-element.15.sum_a, ...), custom_call_target="tpu_custom_call" | custom-call | tf_op jit(solution)/shard_map/finish/pallas_call | solution.py:862

commit v6 on v5

--- a/solution.py
+++ b/solution.py
@@ -543,8 +543,6 @@
     keep[0].start()
     sent_cot = exchange_z(turned, lambda slot: cot_rows.at[:, lanes(slot)])
     normed_ring.share_back()
-    attended_ring.share_back()
-    attended_ring.share_far()
     normed_ring.end()
 
     def multiply(grads, part, width):
@@ -625,6 +623,8 @@
 
     wait_all(sent_query + sent_values)
     sent_a = scatter(grads_a, part_a, 2 * HEAD, x_first_a, z_first_a)
+    attended_ring.share_back()
+    attended_ring.share_far()
 
     wait_all(sent_keys)
     sent_b = scatter(grads_b, part_b, HEAD, x_first_b, z_first_b)

time: 85.7 us -> 85.7 us (level)
  no operation moved by 1% of the time
where the time goes in v6:
time: 85.7 us; the launch traced here: 85.6 us
  Pallas kernels  84.9 us (99%)
    pallas_call x1, Pallas kernels, whole_layer(): pl.pallas_call(layer_kernel, out_shape=(jax.ShapeDtypeStruct(full, BF16),...  82.5 us
    pallas_call x1, Pallas kernels, finish(): pl.pallas_call(functools.partial(finish_kernel, factor), grid=(steps,), o...  2.47 us

profile of v6, /device:TPU:1, one launch (start us, length us, event | category | flops | bytes accessed | tf_op | source)
XLA Modules:
  0.0 85.6 jit_solution(11546286236176309262)
XLA Ops:
  0.6 82.5 %whole_layer.1 = (bf16[128,2048]{1,0:T(8,128)(2,1)}, bf16[128,2048]{1,0:T(8,128)(2,1)}, bf16[64,2048]{1,0:T(8,128)(2,1)}, bf16[64,1024]{1,0:T(8,128)(2,1)}, bf16[64,1024]{1,0:T(8,128)(2,1)}) custom-call(bf16[128,2048]{1,0:T(8,128)(2,1)} %bitcast.5, bf16[128,2048]{1,0:T(8,128)(2,1)} %bitcast.6, bf16[2048,3072]{1,0:T(8,128)(2,1)} %w_qkv_hbm.1, ...), custom_call_target="tpu_custom_call" | custom-call | tf_op jit(solution)/shard_map/whole_layer/pallas_call | solution.py:808
  83.1 2.5 %finish.1 = (bf16[128,2048]{1,0:T(8,128)(2,1)}, bf16[128,2048]{1,0:T(8,128)(2,1)}, f32[64,3072]{1,0:T(8,128)}, f32[64,1024]{1,0:T(8,128)}) custom-call(bf16[128,2048]{1,0:T(8,128)(2,1)} %get-tuple-element.13.layer_in, bf16[128,2048]{1,0:T(8,128)(2,1)} %get-tuple-element.14.tokens_in, bf16[64,2048]{1,0:T(8,128)(2,1)} %get-tuple-element.15.sum_a, ...), custom_call_target="tpu_custom_call" | custom-call | tf_op jit(solution)/shard_map/finish/pallas_call | solution.py:862

commit v7 on v4

--- a/solution.py
+++ b/solution.py
@@ -134,11 +134,13 @@
     w_out_hbm,
     key_blocks,
     key_count,
-    layer_out,
-    grad_tokens,
+    layer_out_hbm,
+    grad_tokens_hbm,
     sum_a,
     sum_b,
     sum_out,
+    layer_out,
+    grad_tokens,
     tokens,
     upstream,
     w_query,
@@ -520,6 +522,11 @@
         return carry
 
     lax.fori_loop(0, D // WIDE, out_chunk, 0)
+    stored = [
+        pltpu.make_async_copy(layer_out, layer_out_hbm, local.at[13]),
+        pltpu.make_async_copy(grad_tokens, grad_tokens_hbm, local.at[14]),
+    ]
+    stored[0].start()
     take_back(pair_count)
     settle(grad_values, INNER)
     sent_values = swap_columns(grad_values, grads_a, pl.ds(HEAD, HEAD), 8)
@@ -680,6 +687,7 @@
         for o in STEPS
     ]
     lax.fori_loop(0, D // WIDE, tokens_chunk, 0)
+    stored[1].start()
     then_b = scatter_on(
         sent_b, part_b, x_first_b, z_first_b, x_summed_b, z_summed_b, then_z_b, then_x_b
     )
@@ -740,7 +748,7 @@
         def _(incoming=incoming):
             incoming.wait_recv()
 
-    wait_all(last)
+    wait_all(last + stored)
 
 
 def whole_layer(tokens, upstream, w_qkv, w_out, key_blocks, key_count):
@@ -749,6 +757,8 @@
     full = (TOK_DEV, D)
     weight = (D, INNER)
     scratch = [
+        (full, BF16),
+        (full, BF16),
         (full, BF16),
         (full, BF16),
         (weight, BF16),
@@ -815,12 +825,12 @@
             jax.ShapeDtypeStruct((ROWS, INNER), BF16),
         ),
         in_specs=[anywhere] * 4 + [scalars] * 2,
-        out_specs=(vector,) * 5,
+        out_specs=(anywhere,) * 2 + (vector,) * 3,
         scratch_shapes=[pltpu.VMEM(shape, dtype) for shape, dtype in scratch]
         + [
             pltpu.SemaphoreType.DMA((semaphores,)),
             pltpu.SemaphoreType.DMA((semaphores,)),
-            pltpu.SemaphoreType.DMA((13,)),
+            pltpu.SemaphoreType.DMA((15,)),
         ],
         compiler_params=pltpu.CompilerParams(
             collective_id=0, has_side_effects=True, vmem_limit_bytes=VMEM_LIMIT

time: 85.7 us -> 85.4 us (level)
  no operation moved by 1% of the time
where the time goes in v7:
time: 85.4 us; the launch traced here: 85.2 us
  Pallas kernels  84.6 us (99%)
    pallas_call x1, Pallas kernels, whole_layer(): pl.pallas_call(layer_kernel, out_shape=(jax.ShapeDtypeStruct(full, BF16),...  82.1 us
    pallas_call x1, Pallas kernels, finish(): pl.pallas_call(functools.partial(finish_kernel, factor), grid=(steps,), o...  2.47 us

profile of v7, /device:TPU:1, one launch (start us, length us, event | category | flops | bytes accessed | tf_op | source)
XLA Modules:
  0.0 85.2 jit_solution(1530715843314614328)
XLA Ops:
  0.6 82.1 %whole_layer.1 = (bf16[128,2048]{1,0:T(8,128)(2,1)}, bf16[128,2048]{1,0:T(8,128)(2,1)}, bf16[64,2048]{1,0:T(8,128)(2,1)}, bf16[64,1024]{1,0:T(8,128)(2,1)}, bf16[64,1024]{1,0:T(8,128)(2,1)}) custom-call(bf16[128,2048]{1,0:T(8,128)(2,1)} %bitcast.5, bf16[128,2048]{1,0:T(8,128)(2,1)} %bitcast.6, bf16[2048,3072]{1,0:T(8,128)(2,1)} %w_qkv_hbm.1, ...), custom_call_target="tpu_custom_call" | custom-call | tf_op jit(solution)/shard_map/whole_layer/pallas_call | solution.py:818
  82.7 2.5 %finish.1 = (bf16[128,2048]{1,0:T(8,128)(2,1)}, bf16[128,2048]{1,0:T(8,128)(2,1)}, f32[64,3072]{1,0:T(8,128)}, f32[64,1024]{1,0:T(8,128)}) custom-call(bf16[128,2048]{1,0:T(8,128)(2,1)} %get-tuple-element.13.layer_in, bf16[128,2048]{1,0:T(8,128)(2,1)} %get-tuple-element.14.tokens_in, bf16[64,2048]{1,0:T(8,128)(2,1)} %get-tuple-element.15.sum_a, ...), custom_call_target="tpu_custom_call" | custom-call | tf_op jit(solution)/shard_map/finish/pallas_call | solution.py:872

commit v8 on v4

--- a/solution.py
+++ b/solution.py
@@ -479,7 +479,6 @@
     lax.fori_loop(0, pair_count, pairs(weigh), 0)
     normed_ring.pass_on()
     take_halo(1)
-    normed_ring.begin_slow(1)
 
     def attend_pair(i, carry):
         pairs(attend)(i, carry)
@@ -521,6 +520,7 @@
 
     lax.fori_loop(0, D // WIDE, out_chunk, 0)
     take_back(pair_count)
+    normed_ring.begin_slow(1)
     settle(grad_values, INNER)
     sent_values = swap_columns(grad_values, grads_a, pl.ds(HEAD, HEAD), 8)
     attended_ring.pass_on()

time: 85.7 us -> 90.4 us (1.055)
  Pallas kernels: 84.9 us -> 89.6 us
    pallas_call x1, Pallas kernels: 82.4 us -> 87.2 us  [whole_layer(): pl.pallas_call(layer_kernel, out_shape=(jax.ShapeDtypeStruct(full, BF16),...]
where the time goes in v8:
time: 90.4 us; the launch traced here: 90.3 us
  Pallas kernels  89.6 us (99%)
    pallas_call x1, Pallas kernels, whole_layer(): pl.pallas_call(layer_kernel, out_shape=(jax.ShapeDtypeStruct(full, BF16),...  87.2 us
    pallas_call x1, Pallas kernels, finish(): pl.pallas_call(functools.partial(finish_kernel, factor), grid=(steps,), o...  2.47 us

profile of v8, /device:TPU:1, one launch (start us, length us, event | category | flops | bytes accessed | tf_op | source)
XLA Modules:
  0.0 90.3 jit_solution(1709982951440350875)
XLA Ops:
  0.6 87.2 %whole_layer.1 = (bf16[128,2048]{1,0:T(8,128)(2,1)}, bf16[128,2048]{1,0:T(8,128)(2,1)}, bf16[64,2048]{1,0:T(8,128)(2,1)}, bf16[64,1024]{1,0:T(8,128)(2,1)}, bf16[64,1024]{1,0:T(8,128)(2,1)}) custom-call(bf16[128,2048]{1,0:T(8,128)(2,1)} %bitcast.5, bf16[128,2048]{1,0:T(8,128)(2,1)} %bitcast.6, bf16[2048,3072]{1,0:T(8,128)(2,1)} %w_qkv_hbm.1, ...), custom_call_target="tpu_custom_call" | custom-call | tf_op jit(solution)/shard_map/whole_layer/pallas_call | solution.py:808
  87.8 2.5 %finish.1 = (bf16[128,2048]{1,0:T(8,128)(2,1)}, bf16[128,2048]{1,0:T(8,128)(2,1)}, f32[64,3072]{1,0:T(8,128)}, f32[64,1024]{1,0:T(8,128)}) custom-call(bf16[128,2048]{1,0:T(8,128)(2,1)} %get-tuple-element.13.layer_in, bf16[128,2048]{1,0:T(8,128)(2,1)} %get-tuple-element.14.tokens_in, bf16[64,2048]{1,0:T(8,128)(2,1)} %get-tuple-element.15.sum_a, ...), custom_call_target="tpu_custom_call" | custom-call | tf_op jit(solution)/shard_map/finish/pallas_call | solution.py:862
